TPU v7x, 256 devices: a whole 4x4x8 slice. The times are simulated.
256 devices in a mesh: ctx: 32 (over z_lo, x, core), ch: 8 (over z_hi, y).
Axes of the slice: x: 4, y: 4, z: 8 (z_hi: 2, z_lo: 4; z = z_hi * 4 + z_lo), core: 2. Of those that a mesh axis runs over, the one named last changes fastest.
Arguments:
- q_stream: bfloat16 [4096, 4096], P('ch', 'ctx'), may hold values from -6 to 6
- k_stream: bfloat16 [4096, 4096], P('ch', 'ctx'), may hold values from -6 to 6
- x_stream: bfloat16 [4096, 4096], P('ch', 'ctx'), may hold values from -6 to 6
- short_taps: float32 [3, 3, 4096], P(None, None, 'ch'), may hold values from -3 to 3
- skip_gain: float32 [4096], P('ch'), may hold values from -4 to 4
- filter_taps: bfloat16 [256, 4096], P('ch', 'ctx'), may hold values from -0.375 to 0.375
Outputs:
- mixed: bfloat16 [4096, 4096], P('ch', 'ctx')
All inputs are finite; a program needn't handle non-finite values.
Results may differ from a plain program's by a relative error of at most 0.0049.
Values may be sent and summed in bfloat16 or wider, within the bound.
No kernel may reach another device: no remote copies, remote signals or barrier semaphores. Data moves between devices by JAX's collectives and lax.ppermute only.
A program may use at most 64 MiB of HBM per device.

v0:
```python
import jax
import jax.numpy as jnp
from jax import lax
from jax.sharding import PartitionSpec as P

LAG_BLOCK = 4


def passed_along(shard, axis, by):
    length = lax.axis_size(axis)
    pairs = [(i, i + by) for i in range(length) if 0 <= i + by < length]
    return lax.ppermute(shard, axis, pairs)


def short_conv(stream, before, weights):
    joined = jnp.concatenate([before, stream], axis=1).astype(jnp.float32)
    length = stream.shape[1]
    return (
        weights[0][:, None] * joined[:, 2:]
        + weights[1][:, None] * joined[:, 1 : length + 1]
        + weights[2][:, None] * joined[:, 0:length]
    )


def pad_lags(taps, stretch_rows):
    return jnp.concatenate([jnp.zeros((taps.shape[0], stretch_rows), taps.dtype), taps], axis=1)


def lag_table(padded, first_lag, stretch_rows):
    group_count = padded.shape[0]
    span = (LAG_BLOCK + 1) * stretch_rows
    segment = lax.dynamic_slice_in_dim(
        padded, (first_lag * stretch_rows).astype(jnp.int32), span, 1
    )
    rolled = jnp.concatenate([segment[:, stretch_rows:], segment[:, :stretch_rows]], axis=1)
    tiled = jnp.tile(rolled, (1, stretch_rows))
    skewed = tiled[:, : stretch_rows * (span - 1)].reshape(group_count, stretch_rows, span - 1)
    return skewed[:, :, : LAG_BLOCK * stretch_rows].reshape(
        group_count, stretch_rows, LAG_BLOCK, stretch_rows
    )


def body(q_stream, k_stream, x_stream, short_taps, skip_gain, filter_taps):
    channels, stretch_rows = q_stream.shape
    devices = lax.axis_size("ctx")
    before = passed_along((q_stream[:, -2:], k_stream[:, -2:], x_stream[:, -2:]), "ctx", 1)
    q_short = short_conv(q_stream, before[0], short_taps[0])
    k_short = short_conv(k_stream, before[1], short_taps[1])
    x_short = short_conv(x_stream, before[2], short_taps[2])
    gated = (k_short * x_short).astype(jnp.bfloat16)
    slice_rows, taps_slice = (
        lax.all_to_all(gated, "ctx", split_axis=0, concat_axis=1, tiled=True),
        lax.all_to_all(filter_taps, "ctx", split_axis=0, concat_axis=1, tiled=True),
    )
    group_count = taps_slice.shape[0]
    group_width = slice_rows.shape[0] // group_count
    padded = pad_lags(taps_slice, stretch_rows)
    widened = jnp.concatenate([jnp.zeros_like(slice_rows), slice_rows], axis=1)
    blocks = widened.reshape(group_count, group_width, 2 * devices, stretch_rows)

    def turn(step, total):
        first_lag = step * LAG_BLOCK
        table = lag_table(padded, first_lag, stretch_rows)
        views = [
            lax.dynamic_slice_in_dim(
                blocks, (devices - first_lag - k).astype(jnp.int32), devices, 2
            )
            for k in range(LAG_BLOCK)
        ]
        window = jnp.stack(views, axis=2)
        return total + jnp.einsum(
            "gskt,gwkrs->gwrt", table, window, preferred_element_type=jnp.float32
        )

    start_total = jnp.zeros((group_count, group_width, devices, stretch_rows), jnp.float32)
    parts = lax.fori_loop(0, devices // LAG_BLOCK, turn, start_total)
    returned = lax.all_to_all(parts, "ctx", split_axis=2, concat_axis=0, tiled=True)
    filtered = returned.reshape(channels, stretch_rows)
    mixed = q_short * (filtered + skip_gain[:, None] * gated.astype(jnp.float32))
    return mixed.astype(jnp.bfloat16)


def solution(mesh):
    return jax.shard_map(
        body,
        mesh=mesh,
        in_specs=(
            P("ch", "ctx"),
            P("ch", "ctx"),
            P("ch", "ctx"),
            P(None, None, "ch"),
            P("ch"),
            P("ch", "ctx"),
        ),
        out_specs=P("ch", "ctx"),
        check_vma=False,
    )
```

profile of v0, /device:TPU:1, one launch (start us, length us, event | category | flops | bytes accessed | tf_op | source)
XLA Modules:
  0.0 75.7 jit_solution(3629845807758044661)
XLA Ops:
  0.0 1.0 %slice.144 = bf16[512,2]{1,0:T(8,128)(2,1)S(1)} slice(bf16[512,128]{1,0:T(8,128)(2,1)} %param.9), slice={[0:512], [126:128]} | slice | bytes 4096 | tf_op jit(solution)/shard_map/slice | solution.py:46
  1.1 4.6 %collective-permute-start.1 = (bf16[512,2]{1,0:T(8,128)(2,1)S(1)}, bf16[512,2]{1,0:T(8,128)(2,1)S(1)}, u32[]{:S(2)}, u32[]{:S(2)}) collective-permute-start(bf16[512,2]{1,0:T(8,128)(2,1)S(1)} %slice.144), channel_id=1, source_target_pairs={{0,8},{8,16},{16,24},{24,32},{32,40},{40,48},{48,56},{56,64},{64,7... | collective-permute-start | bytes 6152 | tf_op jit(solution)/shard_map/ppermute | solution.py:12
  5.8 1.9 %collective-permute-start.2 = (bf16[512,2]{1,0:T(8,128)(2,1)S(1)}, bf16[512,2]{1,0:T(8,128)(2,1)S(1)}, u32[]{:S(2)}, u32[]{:S(2)}) collective-permute-start(bf16[512,2]{1,0:T(8,128)(2,1)S(1)} %slice.151), channel_id=1, source_target_pairs={{0,8},{8,16},{16,24},{24,32},{32,40},{40,48},{48,56},{56,64},{64,7... | collective-permute-start | bytes 6152 | tf_op jit(solution)/shard_map/ppermute | solution.py:12
  8.4 8.7 %all-to-all-start.1 = ((bf16[32,1,128]{2,1,0:T(2,128)(2,1)}), bf16[32,1,128]{2,1,0:T(2,128)(2,1)S(1)}, u32[]{:S(2)}, u32[]{:S(2)}) async-start(bf16[32,1,128]{2,1,0:T(2,128)(2,1)} %copy.22), calls=%async_computation.1 | async-start | bytes 32768 | tf_op jit(solution)/shard_map/all_to_all | solution.py:53
  17.5 1.4 %fusion.10 = bf16[512,128]{1,0:T(8,128)(2,1)} fusion(f32[512,130]{1,0:T(8,128)S(1)} %maximum_convert_fusion.2, f32[512,130]{1,0:T(8,128)S(1)} %maximum_convert_fusion.1, f32[512]{0:T(512)S(1)} %bitcast.80, f32[512]{0:T(512)S(1)} %bitcast.81, f32[512]{0:T(512)S(1)} %bitcast.76, f32[512]{0:T(512)S(1)} %bitcast.77, f32[512]{0:T(512)S(1)} %bitcast.78, ...), kind=kLoop, calls=%fused_computation.22 | loop fusion | flops 786432 | bytes 1716224 | tf_op jit(solution)/shard_map/convert_element_type | solution.py:50
  18.9 5.6 %all-to-all-done.1 = bf16[32,1,128]{2,1,0:T(2,128)(2,1)S(1)} async-done(((bf16[32,1,128]{2,1,0:T(2,128)(2,1)}), bf16[32,1,128]{2,1,0:T(2,128)(2,1)S(1)}, u32[]{:S(2)}, u32[]{:S(2)}) %all-to-all-start.1) | async-done | bytes 8224 | tf_op jit(solution)/shard_map/all_to_all | solution.py:53
  24.5 4.2 %all-to-all-start = ((bf16[32,16,128]{2,1,0:T(8,128)(2,1)}), bf16[32,16,128]{2,1,0:T(8,128)(2,1)S(1)}, u32[]{:S(2)}, u32[]{:S(2)}) async-start(bf16[32,16,128]{2,1,0:T(8,128)(2,1)} %bitcast.9), calls=%async_computation | async-start | bytes 262144 | tf_op jit(solution)/shard_map/all_to_all | solution.py:52
  28.6 8.6 %all-to-all-done = bf16[32,16,128]{2,1,0:T(8,128)(2,1)S(1)} async-done(((bf16[32,16,128]{2,1,0:T(8,128)(2,1)}), bf16[32,16,128]{2,1,0:T(8,128)(2,1)S(1)}, u32[]{:S(2)}, u32[]{:S(2)}) %all-to-all-start) | async-done | bytes 131104 | tf_op jit(solution)/shard_map/all_to_all | solution.py:52
  37.3 19.7 %while.18 = (s32[]{:T(128)}, f32[1,16,32,128]{3,2,1,0:T(8,128)S(1)}, bf16[1,16,64,128]{3,2,1,0:T(8,128)(2,1)S(1)}, bf16[1,4224]{1,0:T(2,128)(2,1)S(1)}, s32[]{:T...) while((s32[]{:T(128)}, ...), condition=%wide.region_1.0_spmd.clone, body=%wide.region_0.0_spmd.clone.sunk | while | flops 68028952 | bytes 3905221 | solution.py:76
  38.0 0.9 %slice_reduce_fusion.2 = bf16[81792]{0:T(1024)(128)(2,1)S(1)} fusion(bf16[1,81920]{1,0:T(2,128)(2,1)S(1)} %bitcast.69), kind=kLoop, calls=%fused_computation.9.clone.1 | loop fusion | bytes 327168 | tf_op jit(solution)/shard_map/while/body/eval_jaxpr/slice | solution.py:37
  40.4 0.9 %slice_reduce_fusion.2 = bf16[81792]{0:T(1024)(128)(2,1)S(1)} fusion(bf16[1,81920]{1,0:T(2,128)(2,1)S(1)} %bitcast.69), kind=kLoop, calls=%fused_computation.9.clone.1 | loop fusion | bytes 327168 | tf_op jit(solution)/shard_map/while/body/eval_jaxpr/slice | solution.py:37
  42.9 0.9 %slice_reduce_fusion.2 = bf16[81792]{0:T(1024)(128)(2,1)S(1)} fusion(bf16[1,81920]{1,0:T(2,128)(2,1)S(1)} %bitcast.69), kind=kLoop, calls=%fused_computation.9.clone.1 | loop fusion | bytes 327168 | tf_op jit(solution)/shard_map/while/body/eval_jaxpr/slice | solution.py:37
  45.3 0.9 %slice_reduce_fusion.2 = bf16[81792]{0:T(1024)(128)(2,1)S(1)} fusion(bf16[1,81920]{1,0:T(2,128)(2,1)S(1)} %bitcast.69), kind=kLoop, calls=%fused_computation.9.clone.1 | loop fusion | bytes 327168 | tf_op jit(solution)/shard_map/while/body/eval_jaxpr/slice | solution.py:37
  47.8 0.9 %slice_reduce_fusion.2 = bf16[81792]{0:T(1024)(128)(2,1)S(1)} fusion(bf16[1,81920]{1,0:T(2,128)(2,1)S(1)} %bitcast.69), kind=kLoop, calls=%fused_computation.9.clone.1 | loop fusion | bytes 327168 | tf_op jit(solution)/shard_map/while/body/eval_jaxpr/slice | solution.py:37
  50.2 0.9 %slice_reduce_fusion.2 = bf16[81792]{0:T(1024)(128)(2,1)S(1)} fusion(bf16[1,81920]{1,0:T(2,128)(2,1)S(1)} %bitcast.69), kind=kLoop, calls=%fused_computation.9.clone.1 | loop fusion | bytes 327168 | tf_op jit(solution)/shard_map/while/body/eval_jaxpr/slice | solution.py:37
  52.7 0.9 %slice_reduce_fusion.2 = bf16[81792]{0:T(1024)(128)(2,1)S(1)} fusion(bf16[1,81920]{1,0:T(2,128)(2,1)S(1)} %bitcast.69), kind=kLoop, calls=%fused_computation.9.clone.1 | loop fusion | bytes 327168 | tf_op jit(solution)/shard_map/while/body/eval_jaxpr/slice | solution.py:37
  55.2 0.9 %slice_reduce_fusion.2 = bf16[81792]{0:T(1024)(128)(2,1)S(1)} fusion(bf16[1,81920]{1,0:T(2,128)(2,1)S(1)} %bitcast.69), kind=kLoop, calls=%fused_computation.9.clone.1 | loop fusion | bytes 327168 | tf_op jit(solution)/shard_map/while/body/eval_jaxpr/slice | solution.py:37
  57.0 0.9 %copy.23 = f32[1,16,32,128]{3,1,0,2:T(8,128)} copy(f32[1,16,32,128]{3,2,1,0:T(8,128)S(1)} %get-tuple-element.152) | data formatting | bytes 524288 | tf_op jit(solution)/shard_map/while | solution.py:76
  57.9 3.9 %all-to-all-start.2 = ((f32[1,16,32,128]{3,1,0,2:T(8,128)}), f32[1,16,32,128]{3,1,0,2:T(8,128)S(1)}, u32[]{:S(2)}, u32[]{:S(2)}) async-start(f32[1,16,32,128]{3,1,0,2:T(8,128)} %copy.23), calls=%async_computation.2 | async-start | bytes 524288 | tf_op jit(solution)/shard_map/all_to_all | solution.py:77
  61.9 3.5 %collective-permute-start = (bf16[512,2]{1,0:T(8,128)(2,1)S(1)}, bf16[512,2]{1,0:T(8,128)(2,1)S(1)}, u32[]{:S(2)}, u32[]{:S(2)}) collective-permute-start(bf16[512,2]{1,0:T(8,128)(2,1)S(1)} %slice.137), channel_id=1, source_target_pairs={{0,8},{8,16},{16,24},{24,32},{32,40},{40,48},{48,56},{56,64},{64,7... | collective-permute-start | bytes 6152 | tf_op jit(solution)/shard_map/ppermute | solution.py:12
  65.5 2.2 %collective-permute-done = bf16[512,2]{1,0:T(8,128)(2,1)S(1)} collective-permute-done((bf16[512,2]{1,0:T(8,128)(2,1)S(1)}, bf16[512,2]{1,0:T(8,128)(2,1)S(1)}, u32[]{:S(2)}, u32[]{:S(2)}) %collective-permute-start) | collective-permute-done | bytes 2080 | tf_op jit(solution)/shard_map/ppermute | solution.py:12
  67.8 5.2 %all-to-all-done.2 = f32[1,16,32,128]{3,1,0,2:T(8,128)S(1)} async-done(((f32[1,16,32,128]{3,1,0,2:T(8,128)}), f32[1,16,32,128]{3,1,0,2:T(8,128)S(1)}, u32[]{:S(2)}, u32[]{:S(2)}) %all-to-all-start.2) | async-done | bytes 262176 | tf_op jit(solution)/shard_map/all_to_all | solution.py:77
  73.0 0.7 copy-done.5
  73.7 2.0 %fusion.16 = bf16[512,128]{1,0:T(8,128)(2,1)} fusion(f32[512,130]{1,0:T(8,128)S(1)} %maximum_convert_fusion, f32[1,16,32,128]{3,1,0,2:T(8,128)S(1)} %all-to-all-done.2, bf16[512,128]{1,0:T(8,128)(2,1)} %fusion.10, f32[512]{0:T(512)S(1)} %copy-done.5, f32[512]{0:T(512)S(1)} %bitcast.74, f32[512]{0:T(512)S(1)} %bitcast.75, f32[512]{0:T(512)S(1)} %bitcast.73), kind=kLoop, calls=%fused_computation.34 | loop fusion | flops 655360 | bytes 1318912 | tf_op jit(solution)/shard_map/convert_element_type | solution.py:80
  (105 shorter events, 12.8 us)
Async XLA Ops:
  0.0 5.7 %copy-start.1 = (bf16[512,128]{1,0:T(8,128)(2,1)S(1)}, bf16[512,128]{1,0:T(8,128)(2,1)}, u32[]{:S(2)}) copy-start(bf16[512,128]{1,0:T(8,128)(2,1)} %param.10) | copy-start | bytes 393220
  1.0 6.7 %copy-start.4 = (bf16[32,128]{1,0:T(8,128)(2,1)S(1)}, bf16[32,128]{1,0:T(8,128)(2,1)}, u32[]{:S(2)}) copy-start(bf16[32,128]{1,0:T(8,128)(2,1)} %param.13) | copy-start | bytes 24580
  1.1 16.1 %copy-start = (bf16[512,128]{1,0:T(8,128)(2,1)S(1)}, bf16[512,128]{1,0:T(8,128)(2,1)}, u32[]{:S(2)}) copy-start(bf16[512,128]{1,0:T(8,128)(2,1)} %param.9) | copy-start | bytes 393220
  1.1 16.1 %collective-permute-start.1 = (bf16[512,2]{1,0:T(8,128)(2,1)S(1)}, bf16[512,2]{1,0:T(8,128)(2,1)S(1)}, u32[]{:S(2)}, u32[]{:S(2)}) collective-permute-start(bf16[512,2]{1,0:T(8,128)(2,1)S(1)} %slice.144), channel_id=1, source_target_pairs={{0,8},{8,16},{16,24},{24,32},{32,40},{40,48},{48,56},{56,64},{64,7... | collective-permute-start | bytes 6152 | tf_op jit(solution)/shard_map/ppermute | solution.py:12
  5.8 11.5 %collective-permute-start.2 = (bf16[512,2]{1,0:T(8,128)(2,1)S(1)}, bf16[512,2]{1,0:T(8,128)(2,1)S(1)}, u32[]{:S(2)}, u32[]{:S(2)}) collective-permute-start(bf16[512,2]{1,0:T(8,128)(2,1)S(1)} %slice.151), channel_id=1, source_target_pairs={{0,8},{8,16},{16,24},{24,32},{32,40},{40,48},{48,56},{56,64},{64,7... | collective-permute-start | bytes 6152 | tf_op jit(solution)/shard_map/ppermute | solution.py:12
  7.8 9.3 %copy-start.3 = (f32[3,3,512]{2,1,0:T(4,128)S(1)}, f32[3,3,512]{2,1,0:T(4,128)}, u32[]{:S(2)}) copy-start(f32[3,3,512]{2,1,0:T(4,128)} %param.11) | copy-start | bytes 55300
  8.4 16.1 %all-to-all-start.1 = ((bf16[32,1,128]{2,1,0:T(2,128)(2,1)}), bf16[32,1,128]{2,1,0:T(2,128)(2,1)S(1)}, u32[]{:S(2)}, u32[]{:S(2)}) async-start(bf16[32,1,128]{2,1,0:T(2,128)(2,1)} %copy.22), calls=%async_computation.1 | async-start | bytes 32768 | tf_op jit(solution)/shard_map/all_to_all | solution.py:53
  24.5 12.8 %all-to-all-start = ((bf16[32,16,128]{2,1,0:T(8,128)(2,1)}), bf16[32,16,128]{2,1,0:T(8,128)(2,1)S(1)}, u32[]{:S(2)}, u32[]{:S(2)}) async-start(bf16[32,16,128]{2,1,0:T(8,128)(2,1)} %bitcast.9), calls=%async_computation | async-start | bytes 262144 | tf_op jit(solution)/shard_map/all_to_all | solution.py:52
  57.9 4.0 %copy-start.2 = (bf16[512,128]{1,0:T(8,128)(2,1)S(1)}, bf16[512,128]{1,0:T(8,128)(2,1)}, u32[]{:S(2)}) copy-start(bf16[512,128]{1,0:T(8,128)(2,1)} %param.8) | copy-start | bytes 393220
  57.9 15.1 %all-to-all-start.2 = ((f32[1,16,32,128]{3,1,0,2:T(8,128)}), f32[1,16,32,128]{3,1,0,2:T(8,128)S(1)}, u32[]{:S(2)}, u32[]{:S(2)}) async-start(f32[1,16,32,128]{3,1,0,2:T(8,128)} %copy.23), calls=%async_computation.2 | async-start | bytes 524288 | tf_op jit(solution)/shard_map/all_to_all | solution.py:77
  61.9 5.8 %collective-permute-start = (bf16[512,2]{1,0:T(8,128)(2,1)S(1)}, bf16[512,2]{1,0:T(8,128)(2,1)S(1)}, u32[]{:S(2)}, u32[]{:S(2)}) collective-permute-start(bf16[512,2]{1,0:T(8,128)(2,1)S(1)} %slice.137), channel_id=1, source_target_pairs={{0,8},{8,16},{16,24},{24,32},{32,40},{40,48},{48,56},{56,64},{64,7... | collective-permute-start | bytes 6152 | tf_op jit(solution)/shard_map/ppermute | solution.py:12
  73.0 0.7 copy-start.5
where the time goes:
time: 76.2 us; the launch traced here: 75.7 us
  starting transfers between devices  26.9 us (35%)
  waiting for transfers between devices  21.5 us (28%)
  local copies, waits for them, and re-layouts  19.5 us (26%)
  other arithmetic  4.06 us (5%)
  matrix products  2.61 us (3%)
  loops' own time  0.84 us (1%)
    ppermute x3, starting transfers between devices, passed_along(): return lax.ppermute(shard, axis, pairs)  10.1 us
    all_to_all x1, starting transfers between devices, body(): lax.all_to_all(filter_taps, 'ctx', split_axis=0, concat_axis=1, tiled=True)  8.72 us
    all_to_all x1, waiting for transfers between devices, body(): lax.all_to_all(gated, 'ctx', split_axis=0, concat_axis=1, tiled=True)  8.59 us
    slice x8, local copies, waits for them, and re-layouts, lag_table(): tiled[:, :stretch_rows * (span - 1)]  7.44 us
    all_to_all x1, waiting for transfers between devices, body(): lax.all_to_all(filter_taps, 'ctx', split_axis=0, concat_axis=1, tiled=True)  5.57 us
    all_to_all x1, waiting for transfers between devices, body(): lax.all_to_all(parts, 'ctx', split_axis=2, concat_axis=0, tiled=True)  5.15 us
    all_to_all x1, starting transfers between devices, body(): lax.all_to_all(gated, 'ctx', split_axis=0, concat_axis=1, tiled=True)  4.15 us
    all_to_all x1, starting transfers between devices, body(): lax.all_to_all(parts, 'ctx', split_axis=2, concat_axis=0, tiled=True)  3.95 us
  transfers between devices with their start and end apart: 6, of which 4 were waited for; matrix products, arithmetic and copies ran while one was open for 4% of the time, Pallas kernels for 0%

commit v1 on v0

v1 whole, which is shorter than its diff:
```python
import jax
import jax.numpy as jnp
from jax import lax
from jax.experimental import pallas as pl
from jax.experimental.pallas import tpu as pltpu
from jax.sharding import PartitionSpec as P

INTERPRET = False
LANES = 128
ROWS = 24
F32 = jnp.float32
BF16 = jnp.bfloat16


def iota(shape, dim):
    return lax.broadcasted_iota(jnp.int32, shape, dim)


def one_hot(mask):
    return jnp.where(mask, 1.0, 0.0).astype(BF16)


def dot(a, b):
    return jnp.dot(a, b, preferred_element_type=F32)


def tap_columns(taps_ref, streams):
    rows = [taps_ref[m] for m in streams]
    count = 3 * len(streams)
    rows.append(jnp.zeros((8 - count, taps_ref.shape[2]), F32))
    return jnp.concatenate(rows, axis=0).T


def pack_kernel(k_ref, x_ref, taps_ref, lags_ref, out_ref):
    channels, length = k_ref.shape
    parts = lags_ref.shape[0]
    width = channels // parts
    columns = tap_columns(taps_ref, (1, 2))
    lane = iota((channels, length), 1)

    def short(stream, first):
        one = pltpu.roll(stream, 1, 1)
        two = pltpu.roll(stream, 2, 1)
        return (
            columns[:, first : first + 1] * stream
            + columns[:, first + 1 : first + 2] * one
            + columns[:, first + 2 : first + 3] * two
        )

    k = k_ref[...]
    x = x_ref[...]
    gated = short(k.astype(F32), 0) * short(x.astype(F32), 3)
    gated = jnp.where(lane < 2, 0.0, gated).astype(BF16)
    out_ref[:, 0:width, :] = gated.reshape(parts, width, length)

    src = iota((2 * length, length), 0)
    dst = iota((2 * length, length), 1)
    source_lane = jnp.where(dst % 4 < 2, length - 2 + dst % 4, dst % 4 - 2)
    pick = ((src % length) == source_lane) & ((src >= length) == (dst % 8 >= 4))
    spread = dot(jnp.concatenate([k, x], axis=1), one_hot(pick))
    own = (lane // 8) == (iota((channels, length), 0) % width)
    spread = jnp.where(own, spread, 0.0).astype(BF16)
    tail = 8 * parts
    row = iota((tail, channels), 0)
    gather = one_hot((row % 8 == 1) & (row // 8 == iota((tail, channels), 1) // width))
    row = iota((tail, parts), 0)
    place = one_hot((row % 8 == 0) & (row // 8 == iota((tail, parts), 1)))
    rest = dot(gather, spread) + dot(place, lags_ref[...])
    out_ref[:, width : width + 8, :] = rest.astype(BF16).reshape(parts, 8, length)


def conv_kernel(got_ref, weights_ref, skip_ref, out_ref, table_ref):
    parts, _, length = got_ref.shape
    width = out_ref.shape[1]
    rows = parts * width
    tail = got_ref[:, width : width + 8, :].reshape(8 * parts, length)

    row = iota((8 * parts, 8 * parts), 0)
    col = iota((8 * parts, 8 * parts), 1)
    lags = dot(one_hot((col // 8 == row // 8) & (col % 8 == 0)), tail)
    upper = iota((length, length), 1) >= iota((length, length), 0)
    table_ref[:, 0:length] = jnp.zeros((length, length), BF16)
    before = jnp.zeros((length, length), F32)
    for b in range(parts):
        spread = jnp.concatenate([lags[8 * b : 8 * b + 8]] * (length // 8), axis=0)
        turned = pltpu.roll(spread, 0, 1, stride=1, stride_axis=0)
        table_ref[:, (b + 1) * length : (b + 2) * length] = jnp.where(upper, turned, before).astype(BF16)
        before = turned

    row = iota((parts, 8 * parts), 0)
    col = iota((parts, 8 * parts), 1)
    edge = col % 8 == 1
    own = dot(one_hot(edge & (col // 8 == row)), tail)
    last = dot(one_hot(edge & (col // 8 + 1 == row)), tail)
    lane = iota((parts, length), 1)
    joined = jnp.where(lane % 4 < 2, last, own)
    short = (
        weights_ref[0:1, :] * joined
        + weights_ref[1:2, :] * pltpu.roll(joined, 1, 1)
        + weights_ref[2:3, :] * pltpu.roll(joined, 2, 1)
    )
    first = (short * pltpu.roll(short, length - 4, 1)).astype(BF16)
    row = iota((rows, parts), 0)
    repeated = dot(one_hot(row // width == iota((rows, parts), 1)), first)
    lane = iota((rows, length), 1)
    keep = (lane // 8 == iota((rows, length), 0) % width) & (lane % 8 >= 2) & (lane % 8 < 4)
    repeated = jnp.where(keep, repeated, 0.0).astype(BF16)
    src = iota((length, length), 0)
    dst = iota((length, length), 1)
    fixed = dot(repeated, one_hot((src % 8 - 2 == dst) & (dst < 2)))
    gated = got_ref[:, 0:width, :].reshape(rows, length).astype(F32) + fixed

    pairs = parts // 2
    split = gated.reshape(pairs, 2, width, length)
    even = split[:, 0].reshape(pairs * width, length)
    odd = split[:, 1].reshape(pairs * width, length)
    panel = jnp.concatenate([even, odd], axis=1)
    skip = jnp.concatenate([skip_ref[...]] * 2, axis=1)
    skip = jnp.concatenate([skip] * pairs, axis=0)
    total = panel * skip
    panel = panel.astype(BF16)
    for b in range(pairs):
        at = 2 * b * length
        block = jnp.concatenate(
            [table_ref[:, at + length : at + 3 * length], table_ref[:, at : at + 2 * length]], axis=0
        )
        live = (pairs - b) * width
        term = dot(panel[:live], block)
        if b:
            term = jnp.concatenate([jnp.zeros((b * width, 2 * length), F32), term], axis=0)
        total = total + term
    total = total.astype(BF16)
    halves = [total[:, 0:length], total[:, length:]]
    halves = [h.reshape(pairs, 1, width, length) for h in halves]
    out_ref[...] = jnp.concatenate(halves, axis=1).reshape(parts, width, length)


def mix_kernel(back_ref, q_ref, out_ref):
    parts, width, length = back_ref.shape
    back = back_ref[...].reshape(parts * width, length).astype(F32)
    out_ref[...] = (q_ref[...] * back).astype(BF16)


def call(kernel, out_shape, scratch=()):
    return pl.pallas_call(
        kernel,
        out_shape=out_shape,
        scratch_shapes=list(scratch),
        interpret=INTERPRET,
        name=kernel.__name__,
    )


def short_conv(stream, before, weights):
    joined = jnp.concatenate([before, stream], axis=1).astype(F32)
    length = stream.shape[1]
    return (
        weights[0][:, None] * joined[:, 2:]
        + weights[1][:, None] * joined[:, 1 : length + 1]
        + weights[2][:, None] * joined[:, 0:length]
    )


def body(q_stream, k_stream, x_stream, short_taps, skip_gain, filter_taps):
    channels, length = q_stream.shape
    parts = lax.axis_size("ctx")
    width = channels // parts
    sent = call(pack_kernel, jax.ShapeDtypeStruct((parts, ROWS, length), BF16))(
        k_stream, x_stream, short_taps, filter_taps
    )
    got = lax.all_to_all(sent, "ctx", split_axis=0, concat_axis=0, tiled=True)

    pairs = [(i, i + 1) for i in range(parts - 1)]
    before = lax.ppermute(q_stream[:, -2:], "ctx", pairs)
    q_short = lax.optimization_barrier(short_conv(q_stream, before, short_taps[0]))
    first = lax.axis_index("ctx") * width
    own = lax.dynamic_slice_in_dim(short_taps[1:], first, width, 2)
    own = jnp.repeat(jnp.transpose(own, (1, 2, 0)).reshape(3, 2 * width), 4, axis=1)
    weights = jnp.concatenate([own, jnp.zeros((5, length), F32)], axis=0)
    skip = lax.dynamic_slice_in_dim(skip_gain, first, width, 0)
    skip = jnp.broadcast_to(skip[:, None], (width, length))

    parted = call(
        conv_kernel,
        jax.ShapeDtypeStruct((parts, width, length), BF16),
        [pltpu.VMEM((length, (parts + 1) * length), BF16)],
    )(got, weights, skip)
    back = lax.all_to_all(parted, "ctx", split_axis=0, concat_axis=0, tiled=True)
    return call(mix_kernel, jax.ShapeDtypeStruct((channels, length), BF16))(back, q_short)


def solution(mesh):
    return jax.shard_map(
        body,
        mesh=mesh,
        in_specs=(
            P("ch", "ctx"),
            P("ch", "ctx"),
            P("ch", "ctx"),
            P(None, None, "ch"),
            P("ch"),
            P("ch", "ctx"),
        ),
        out_specs=P("ch", "ctx"),
        check_vma=False,
    )
```

time: 76.2 us -> 40.8 us (0.54)
  local copies, waits for them, and re-layouts: 19.5 us -> 3.93 us
  waiting for transfers between devices: 21.5 us -> 10.6 us
  starting transfers between devices: 26.9 us -> 17.6 us
  Pallas kernels: 0 us -> 6.8 us
  other arithmetic: 4.06 us -> 1.26 us
  matrix products: 2.61 us -> 0 us
  loops' own time: 0.84 us -> 0 us
    slice x43 -> x3, local copies, waits for them, and re-layouts: 9.87 us -> 0.79 us  [the longest x2 0.69 us: body(): own = lax.dynamic_slice_in_dim(short_taps[1:], first, width, 2)]
    all_to_all x3 -> x2, waiting for transfers between devices: 19.3 us -> 10.6 us  [the longest x1 7.24 us: body(): lax.all_to_all(parted, 'ctx', split_axis=0, concat_axis=0, tiled=True)]
    pallas_call x0 -> x3, Pallas kernels: none -> 6.8 us  [the longest x1 2.66 us: body(): call(conv_kernel, jax.ShapeDtypeStruct((parts, width, length), BF16), [pl...]
    ppermute x3 -> x1, starting transfers between devices: 10.1 us -> 3.54 us  [body(): before = lax.ppermute(q_stream[:, -2:], 'ctx', pairs)]
    convert_element_type x5 -> x1, other arithmetic: 3.88 us -> 0.14 us  [short_conv(): joined = jnp.concatenate([before, stream], axis=1).astype(F32)]
    reshape x8 -> x2, local copies, waits for them, and re-layouts: 3.3 us -> 0.21 us  [the longest x1 0.12 us: body(): jnp.repeat(jnp.transpose(own, (1, 2, 0)).reshape(3, 2 * width), 4, axis=1)]
    while x17 -> x0, local copies, waits for them, and re-layouts: 3.04 us -> none
    all_to_all x3 -> x2, starting transfers between devices: 16.8 us -> 14.1 us  [the longest x1 10.1 us: body(): got = lax.all_to_all(sent, 'ctx', split_axis=0, concat_axis=0, tiled=True)]
  transfers between devices with their start and end apart: 6 -> 3, of which waited for: 4 -> 2; matrix products, arithmetic and copies ran while one was open for 4% -> 10% of each run, Pallas kernels for 0% -> 7%
where the time goes in v1:
time: 40.8 us; the launch traced here: 40.3 us
  starting transfers between devices  17.6 us (43%)
  waiting for transfers between devices  10.6 us (26%)
  Pallas kernels  6.8 us (17%)
  local copies, waits for them, and re-layouts  3.93 us (10%)
  other arithmetic  1.26 us (3%)
    all_to_all x1, starting transfers between devices, body(): got = lax.all_to_all(sent, 'ctx', split_axis=0, concat_axis=0, tiled=True)  10.1 us
    all_to_all x1, waiting for transfers between devices, body(): lax.all_to_all(parted, 'ctx', split_axis=0, concat_axis=0, tiled=True)  7.24 us
    all_to_all x1, starting transfers between devices, body(): lax.all_to_all(parted, 'ctx', split_axis=0, concat_axis=0, tiled=True)  3.92 us
    ppermute x1, starting transfers between devices, body(): before = lax.ppermute(q_stream[:, -2:], 'ctx', pairs)  3.54 us
    all_to_all x1, waiting for transfers between devices, body(): got = lax.all_to_all(sent, 'ctx', split_axis=0, concat_axis=0, tiled=True)  3.4 us
    pallas_call x1, Pallas kernels, body(): call(conv_kernel, jax.ShapeDtypeStruct((parts, width, length), BF16), [pl...  2.66 us
    pallas_call x1, Pallas kernels, body(): call(pack_kernel, jax.ShapeDtypeStruct((parts, ROWS, length), BF16))  2.44 us
    pallas_call x1, Pallas kernels, body(): call(mix_kernel, jax.ShapeDtypeStruct((channels, length), BF16))  1.7 us
  transfers between devices with their start and end apart: 3, of which 2 were waited for; matrix products, arithmetic and copies ran while one was open for 10% of the time, Pallas kernels for 7%

profile of v1, /device:TPU:1, one launch (start us, length us, event | category | flops | bytes accessed | tf_op | source)
XLA Modules:
  0.0 40.3 jit_solution(12083199016275366581)
XLA Ops:
  0.0 2.4 %pack_kernel.1 = bf16[32,24,128]{2,1,0:T(8,128)(2,1)} custom-call(bf16[512,128]{1,0:T(8,128)(2,1)} %k_ref.1, bf16[512,128]{1,0:T(8,128)(2,1)} %x_ref.1, f32[3,3,512]{2,1,0:T(4,128)} %taps_ref.1, bf16[32,128]{1,0:T(8,128)(2,1)} %lags_ref.1), custom_call_target="tpu_custom_call" | custom-call | tf_op jit(solution)/shard_map/pack_kernel/pallas_call | solution.py:168
  2.4 10.1 %all-to-all-start = ((bf16[32,24,128]{2,1,0:T(8,128)(2,1)}), bf16[32,24,128]{2,1,0:T(8,128)(2,1)S(1)}, u32[]{:S(2)}, u32[]{:S(2)}) async-start(bf16[32,24,128]{2,1,0:T(8,128)(2,1)} %pack_kernel.1), calls=%async_computation | async-start | bytes 393216 | tf_op jit(solution)/shard_map/all_to_all | solution.py:171
  12.6 0.1 slice.33
  12.7 0.0 copy-start.3
  12.7 3.5 %collective-permute-start = (bf16[512,2]{1,0:T(8,128)(2,1)S(1)}, bf16[512,2]{1,0:T(8,128)(2,1)S(1)}, u32[]{:S(2)}, u32[]{:S(2)}) collective-permute-start(bf16[512,2]{1,0:T(8,128)(2,1)S(1)} %slice.33), channel_id=1, source_target_pairs={{0,8},{8,16},{16,24},{24,32},{32,40},{40,48},{48,56},{56,64},{64,7... | collective-permute-start | bytes 6152 | tf_op jit(solution)/shard_map/ppermute | solution.py:174
  16.3 0.0 slice-start
  16.3 0.7 %slice-done = f32[2,3,512]{2,1,0:T(4,128)S(1)} async-done(((f32[3,3,512]{2,1,0:T(4,128)}), f32[2,3,512]{2,1,0:T(4,128)S(1)}, s32[]{:S(2)}) %slice-start) | async-done | bytes 12312 | tf_op jit(solution)/shard_map/slice | solution.py:177
  17.0 0.1 dynamic-slice_bitcast_fusion
  17.1 0.8 %dynamic_slice.7 = f32[16]{0:T(128)S(1)} dynamic-slice(f32[512]{0:T(512)} %param.10, s32[]{:T(128)S(6)} %select_n.4), dynamic_slice_sizes={16} | dynamic-slice | bytes 132 | tf_op jit(solution)/shard_map/dynamic_slice | solution.py:180
  17.8 0.1 copy.8
  17.9 0.1 reshape.16
  18.0 0.1 broadcast_in_dim.4
  18.1 0.1 reshape.17
  18.2 0.6 %concatenate.6.weights_ref = f32[8,128]{1,0:T(8,128)} pad(f32[3,128]{1,0:T(4,128)S(1)} %reshape.17, f32[]{:T(128)} %constant.13.clone.1), padding=0_5x0_0 | pad | bytes 5636 | tf_op jit(solution)/shard_map/concatenate | solution.py:179
  18.8 3.4 %all-to-all-done.got_ref = bf16[32,24,128]{2,1,0:T(8,128)(2,1)S(1)} async-done(((bf16[32,24,128]{2,1,0:T(8,128)(2,1)}), bf16[32,24,128]{2,1,0:T(8,128)(2,1)S(1)}, u32[]{:S(2)}, u32[]{:S(2)}) %all-to-all-start) | async-done | bytes 196640 | tf_op jit(solution)/shard_map/all_to_all | solution.py:171
  22.2 0.7 %broadcast_in_dim.5.skip_ref = f32[16,128]{1,0:T(8,128)} broadcast(f32[16]{0:T(128)S(1)} %dynamic_slice.7), dimensions={0} | broadcast | bytes 8256 | tf_op jit(solution)/shard_map/broadcast_in_dim | solution.py:181
  22.9 0.0 copy-done
  22.9 2.7 %conv_kernel.1 = bf16[32,16,128]{2,1,0:T(8,128)(2,1)} custom-call(bf16[32,24,128]{2,1,0:T(8,128)(2,1)} %copy-done, f32[8,128]{1,0:T(8,128)} %concatenate.6.weights_ref, f32[16,128]{1,0:T(8,128)} %broadcast_in_dim.5.skip_ref), custom_call_target="tpu_custom_call" | custom-call | tf_op jit(solution)/shard_map/conv_kernel/pallas_call | solution.py:183
  25.5 3.9 %all-to-all-start.1 = ((bf16[32,16,128]{2,1,0:T(8,128)(2,1)}), bf16[32,16,128]{2,1,0:T(8,128)(2,1)S(1)}, u32[]{:S(2)}, u32[]{:S(2)}) async-start(bf16[32,16,128]{2,1,0:T(8,128)(2,1)} %conv_kernel.1), calls=%async_computation.1 | async-start | bytes 262144 | tf_op jit(solution)/shard_map/all_to_all | solution.py:188
  29.5 0.1 maximum_convert_fusion
  29.6 1.1 %fusion.q_ref = f32[512,128]{1,0:T(8,128)} fusion(f32[512,130]{1,0:T(8,128)S(1)} %maximum_convert_fusion, f32[512]{0:T(512)S(1)} %bitcast.6, f32[512]{0:T(512)S(1)} %bitcast.7, f32[512]{0:T(512)S(1)} %bitcast.5), kind=kLoop, calls=%fused_computation.1 | loop fusion | flops 327680 | bytes 1054720 | tf_op jit(solution)/shard_map/add | solution.py:158
  30.7 7.2 %all-to-all-done.1.back_ref = bf16[32,16,128]{2,1,0:T(8,128)(2,1)S(1)} async-done(((bf16[32,16,128]{2,1,0:T(8,128)(2,1)}), bf16[32,16,128]{2,1,0:T(8,128)(2,1)S(1)}, u32[]{:S(2)}, u32[]{:S(2)}) %all-to-all-start.1) | async-done | bytes 131104 | tf_op jit(solution)/shard_map/all_to_all | solution.py:188
  38.0 0.6 %copy-done.2 = bf16[32,16,128]{2,1,0:T(8,128)(2,1)} copy-done((bf16[32,16,128]{2,1,0:T(8,128)(2,1)}, bf16[32,16,128]{2,1,0:T(8,128)(2,1)S(1)}, u32[]{:S(2)}) %copy-start.2) | copy-done | bytes 131096
  38.6 1.7 %mix_kernel.1 = bf16[512,128]{1,0:T(8,128)(2,1)} custom-call(bf16[32,16,128]{2,1,0:T(8,128)(2,1)} %copy-done.2, f32[512,128]{1,0:T(8,128)} %fusion.q_ref), custom_call_target="tpu_custom_call" | custom-call | tf_op jit(solution)/shard_map/mix_kernel/pallas_call | solution.py:189
  (7 shorter events, 0.0 us)
Async XLA Ops:
  2.4 10.1 %copy-start.1 = (bf16[512,128]{1,0:T(8,128)(2,1)S(1)}, bf16[512,128]{1,0:T(8,128)(2,1)}, u32[]{:S(2)}) copy-start(bf16[512,128]{1,0:T(8,128)(2,1)} %param.6) | copy-start | bytes 393220
  2.4 19.8 %all-to-all-start = ((bf16[32,24,128]{2,1,0:T(8,128)(2,1)}), bf16[32,24,128]{2,1,0:T(8,128)(2,1)S(1)}, u32[]{:S(2)}, u32[]{:S(2)}) async-start(bf16[32,24,128]{2,1,0:T(8,128)(2,1)} %pack_kernel.1), calls=%async_computation | async-start | bytes 393216 | tf_op jit(solution)/shard_map/all_to_all | solution.py:171
  12.7 3.6 %copy-start.3 = (f32[3,3,512]{2,1,0:T(4,128)S(1)}, f32[3,3,512]{2,1,0:T(4,128)}, u32[]{:S(2)}) copy-start(f32[3,3,512]{2,1,0:T(4,128)} %taps_ref.1) | copy-start | bytes 55300
  12.7 16.7 %collective-permute-start = (bf16[512,2]{1,0:T(8,128)(2,1)S(1)}, bf16[512,2]{1,0:T(8,128)(2,1)S(1)}, u32[]{:S(2)}, u32[]{:S(2)}) collective-permute-start(bf16[512,2]{1,0:T(8,128)(2,1)S(1)} %slice.33), channel_id=1, source_target_pairs={{0,8},{8,16},{16,24},{24,32},{32,40},{40,48},{48,56},{56,64},{64,7... | collective-permute-start | bytes 6152 | tf_op jit(solution)/shard_map/ppermute | solution.py:174
  16.3 0.7 %slice-start = ((f32[3,3,512]{2,1,0:T(4,128)}), f32[2,3,512]{2,1,0:T(4,128)S(1)}, s32[]{:S(2)}) async-start(f32[3,3,512]{2,1,0:T(4,128)} %taps_ref.1), calls=%async_computation.2 | async-start | bytes 32768 | tf_op jit(solution)/shard_map/slice | solution.py:177
  22.2 0.7 %copy-start = (bf16[32,24,128]{2,1,0:T(8,128)(2,1)}, bf16[32,24,128]{2,1,0:T(8,128)(2,1)S(1)}, u32[]{:S(2)}) copy-start(bf16[32,24,128]{2,1,0:T(8,128)(2,1)S(1)} %all-to-all-done.got_ref) | copy-start | bytes 589828
  25.5 12.4 %all-to-all-start.1 = ((bf16[32,16,128]{2,1,0:T(8,128)(2,1)}), bf16[32,16,128]{2,1,0:T(8,128)(2,1)S(1)}, u32[]{:S(2)}, u32[]{:S(2)}) async-start(bf16[32,16,128]{2,1,0:T(8,128)(2,1)} %conv_kernel.1), calls=%async_computation.1 | async-start | bytes 262144 | tf_op jit(solution)/shard_map/all_to_all | solution.py:188
  38.0 0.6 %copy-start.2 = (bf16[32,16,128]{2,1,0:T(8,128)(2,1)}, bf16[32,16,128]{2,1,0:T(8,128)(2,1)S(1)}, u32[]{:S(2)}) copy-start(bf16[32,16,128]{2,1,0:T(8,128)(2,1)S(1)} %all-to-all-done.1.back_ref) | copy-start | bytes 393220

commit v2 on v1

--- a/solution.py
+++ b/solution.py
@@ -141,14 +141,20 @@
     out_ref[...] = (q_ref[...] * back).astype(BF16)
 
 
-def call(kernel, out_shape, scratch=()):
+def call(kernel, out_shape, scratch=(), near=True):
+    shape, dtype = out_shape
+    out = pltpu.VMEM(shape, dtype) if near and not INTERPRET else jax.ShapeDtypeStruct(shape, dtype)
     return pl.pallas_call(
         kernel,
-        out_shape=out_shape,
+        out_shape=out,
         scratch_shapes=list(scratch),
         interpret=INTERPRET,
         name=kernel.__name__,
     )
+
+
+def near(x):
+    return x if INTERPRET else pltpu.with_memory_space_constraint(x, pltpu.VMEM)
 
 
 def short_conv(stream, before, weights):
@@ -165,7 +171,7 @@
     channels, length = q_stream.shape
     parts = lax.axis_size("ctx")
     width = channels // parts
-    sent = call(pack_kernel, jax.ShapeDtypeStruct((parts, ROWS, length), BF16))(
+    sent = call(pack_kernel, ((parts, ROWS, length), BF16))(
         k_stream, x_stream, short_taps, filter_taps
     )
     got = lax.all_to_all(sent, "ctx", split_axis=0, concat_axis=0, tiled=True)
@@ -182,11 +188,11 @@
 
     parted = call(
         conv_kernel,
-        jax.ShapeDtypeStruct((parts, width, length), BF16),
+        ((parts, width, length), BF16),
         [pltpu.VMEM((length, (parts + 1) * length), BF16)],
-    )(got, weights, skip)
+    )(near(got), near(weights), near(skip))
     back = lax.all_to_all(parted, "ctx", split_axis=0, concat_axis=0, tiled=True)
-    return call(mix_kernel, jax.ShapeDtypeStruct((channels, length), BF16))(back, q_short)
+    return call(mix_kernel, ((channels, length), BF16), near=False)(near(back), near(q_short))
 
 
 def solution(mesh):

time: 40.8 us -> 37.5 us (0.919)
  Pallas kernels: 6.8 us -> 4.84 us
  local copies, waits for them, and re-layouts: 3.93 us -> 2.08 us
  waiting for transfers between devices: 10.6 us -> 11.9 us
  other arithmetic: 1.26 us -> 0.55 us
    pallas_call x3, Pallas kernels: 6.8 us -> 4.84 us  [the longest x1 2.44 us: body(): call(pack_kernel, ((parts, ROWS, length), BF16))]
    add x1, other arithmetic: 1.11 us -> 0.4 us  [short_conv(): weights[0][:, None] * joined[:, 2:]]
    all_to_all x1, waiting for transfers between devices: 7.24 us -> 7.95 us  [body(): lax.all_to_all(parted, 'ctx', split_axis=0, concat_axis=0, tiled=True)]
    unnamed x8 -> x4, local copies, waits for them, and re-layouts: 0.67 us -> 0.01 us
    broadcast_in_dim x1, local copies, waits for them, and re-layouts: 0.67 us -> 0.07 us  [body(): skip = jnp.broadcast_to(skip[:, None], (width, length))]
    concatenate x1, local copies, waits for them, and re-layouts: 0.6 us -> 0.01 us  [body(): weights = jnp.concatenate([own, jnp.zeros((5, length), F32)], axis=0)]
    all_to_all x1, waiting for transfers between devices: 3.4 us -> 3.98 us  [body(): got = lax.all_to_all(sent, 'ctx', split_axis=0, concat_axis=0, tiled=True)]
  transfers between devices with their start and end apart: 3 -> 3, of which waited for: 2 -> 2; matrix products, arithmetic and copies ran while one was open for 10% -> 5% of each run, Pallas kernels for 7% -> 5%
where the time goes in v2:
time: 37.5 us; the launch traced here: 37.1 us
  starting transfers between devices  17.6 us (47%)
  waiting for transfers between devices  11.9 us (32%)
  Pallas kernels  4.84 us (13%)
  local copies, waits for them, and re-layouts  2.08 us (6%)
  other arithmetic  0.55 us (1%)
    all_to_all x1, starting transfers between devices, body(): got = lax.all_to_all(sent, 'ctx', split_axis=0, concat_axis=0, tiled=True)  10.1 us
    all_to_all x1, waiting for transfers between devices, body(): lax.all_to_all(parted, 'ctx', split_axis=0, concat_axis=0, tiled=True)  7.95 us
    all_to_all x1, waiting for transfers between devices, body(): got = lax.all_to_all(sent, 'ctx', split_axis=0, concat_axis=0, tiled=True)  3.98 us
    all_to_all x1, starting transfers between devices, body(): lax.all_to_all(parted, 'ctx', split_axis=0, concat_axis=0, tiled=True)  3.92 us
    ppermute x1, starting transfers between devices, body(): before = lax.ppermute(q_stream[:, -2:], 'ctx', pairs)  3.54 us
    pallas_call x1, Pallas kernels, body(): call(pack_kernel, ((parts, ROWS, length), BF16))  2.44 us
    pallas_call x1, Pallas kernels, body(): call(conv_kernel, ((parts, width, length), BF16), [pltpu.VMEM((length, (p...  1.73 us
    dynamic_slice x1, local copies, waits for them, and re-layouts, body(): skip = lax.dynamic_slice_in_dim(skip_gain, first, width, 0)  0.76 us
  transfers between devices with their start and end apart: 3, of which 2 were waited for; matrix products, arithmetic and copies ran while one was open for 5% of the time, Pallas kernels for 5%

profile of v2, /device:TPU:1, one launch (start us, length us, event | category | flops | bytes accessed | tf_op | source)
XLA Modules:
  0.0 37.1 jit_solution(14135136460580299882)
XLA Ops:
  0.0 2.4 %pack_kernel.1 = bf16[32,24,128]{2,1,0:T(8,128)(2,1)} custom-call(bf16[512,128]{1,0:T(8,128)(2,1)} %k_ref.1, bf16[512,128]{1,0:T(8,128)(2,1)} %x_ref.1, f32[3,3,512]{2,1,0:T(4,128)} %taps_ref.1, bf16[32,128]{1,0:T(8,128)(2,1)} %lags_ref.1), custom_call_target="tpu_custom_call" | custom-call | tf_op jit(solution)/shard_map/pack_kernel/pallas_call | solution.py:174
  2.4 10.1 %all-to-all-start = ((bf16[32,24,128]{2,1,0:T(8,128)(2,1)}), bf16[32,24,128]{2,1,0:T(8,128)(2,1)S(1)}, u32[]{:S(2)}, u32[]{:S(2)}) async-start(bf16[32,24,128]{2,1,0:T(8,128)(2,1)} %pack_kernel.1), calls=%async_computation | async-start | bytes 393216 | tf_op jit(solution)/shard_map/all_to_all | solution.py:177
  12.6 0.0 copy-done
  12.6 0.1 slice.33
  12.7 0.0 copy-start.1
  12.7 3.5 %collective-permute-start = (bf16[512,2]{1,0:T(8,128)(2,1)S(1)}, bf16[512,2]{1,0:T(8,128)(2,1)S(1)}, u32[]{:S(2)}, u32[]{:S(2)}) collective-permute-start(bf16[512,2]{1,0:T(8,128)(2,1)S(1)} %slice.33), channel_id=1, source_target_pairs={{0,8},{8,16},{16,24},{24,32},{32,40},{40,48},{48,56},{56,64},{64,7... | collective-permute-start | bytes 6152 | tf_op jit(solution)/shard_map/ppermute | solution.py:180
  16.3 0.0 slice-start
  16.3 0.0 copy-done.1
  16.3 0.7 %slice-done = f32[2,3,512]{2,1,0:T(4,128)S(1)} async-done(((f32[3,3,512]{2,1,0:T(4,128)}), f32[2,3,512]{2,1,0:T(4,128)S(1)}, s32[]{:S(2)}) %slice-start) | async-done | bytes 12312 | tf_op jit(solution)/shard_map/slice | solution.py:183
  17.0 0.1 dynamic-slice_bitcast_fusion
  17.1 0.8 %dynamic_slice.7 = f32[16]{0:T(128)S(1)} dynamic-slice(f32[512]{0:T(512)} %param.10, s32[]{:T(128)S(6)} %select_n.4), dynamic_slice_sizes={16} | dynamic-slice | bytes 132 | tf_op jit(solution)/shard_map/dynamic_slice | solution.py:186
  17.8 0.1 copy.8
  17.9 0.1 reshape.16
  18.0 0.1 broadcast_in_dim.4
  18.1 0.1 reshape.17
  18.2 4.0 %all-to-all-done.got_ref = bf16[32,24,128]{2,1,0:T(8,128)(2,1)S(1)} async-done(((bf16[32,24,128]{2,1,0:T(8,128)(2,1)}), bf16[32,24,128]{2,1,0:T(8,128)(2,1)S(1)}, u32[]{:S(2)}, u32[]{:S(2)}) %all-to-all-start) | async-done | bytes 196640 | tf_op jit(solution)/shard_map/all_to_all | solution.py:177
  22.2 0.1 broadcast_in_dim.5.skip_ref
  22.3 1.7 %conv_kernel.1 = bf16[32,16,128]{2,1,0:T(8,128)(2,1)} custom-call(bf16[32,24,128]{2,1,0:T(8,128)(2,1)S(1)} %all-to-all-done.got_ref, f32[8,128]{1,0:T(8,128)S(1)} %concatenate.6.weights_ref, f32[16,128]{1,0:T(8,128)S(1)} %broadcast_in_dim.5.skip_ref), custom_call_target="tpu_custom_call" | custom-call | tf_op jit(solution)/shard_map/conv_kernel/pallas_call | solution.py:189
  24.0 3.9 %all-to-all-start.1 = ((bf16[32,16,128]{2,1,0:T(8,128)(2,1)}), bf16[32,16,128]{2,1,0:T(8,128)(2,1)S(1)}, u32[]{:S(2)}, u32[]{:S(2)}) async-start(bf16[32,16,128]{2,1,0:T(8,128)(2,1)} %conv_kernel.1), calls=%async_computation.1 | async-start | bytes 262144 | tf_op jit(solution)/shard_map/all_to_all | solution.py:194
  27.9 0.0 collective-permute-done
  27.9 0.1 maximum_convert_fusion
  28.1 0.4 %fusion.q_ref = f32[512,128]{1,0:T(8,128)S(1)} fusion(f32[512,130]{1,0:T(8,128)S(1)} %maximum_convert_fusion, f32[512]{0:T(512)S(1)} %bitcast.6, f32[512]{0:T(512)S(1)} %bitcast.7, f32[512]{0:T(512)S(1)} %bitcast.5), kind=kLoop, calls=%fused_computation.1 | loop fusion | flops 327680 | bytes 1054720 | tf_op jit(solution)/shard_map/add | solution.py:164
  28.5 7.9 %all-to-all-done.1.back_ref = bf16[32,16,128]{2,1,0:T(8,128)(2,1)S(1)} async-done(((bf16[32,16,128]{2,1,0:T(8,128)(2,1)}), bf16[32,16,128]{2,1,0:T(8,128)(2,1)S(1)}, u32[]{:S(2)}, u32[]{:S(2)}) %all-to-all-start.1) | async-done | bytes 131104 | tf_op jit(solution)/shard_map/all_to_all | solution.py:194
  36.4 0.7 %mix_kernel.1 = bf16[512,128]{1,0:T(8,128)(2,1)} custom-call(bf16[32,16,128]{2,1,0:T(8,128)(2,1)S(1)} %all-to-all-done.1.back_ref, f32[512,128]{1,0:T(8,128)S(1)} %fusion.q_ref), custom_call_target="tpu_custom_call" | custom-call | tf_op jit(solution)/shard_map/mix_kernel/pallas_call | solution.py:195
  (3 shorter events, 0.0 us)
Async XLA Ops:
  2.4 10.1 %copy-start = (bf16[512,128]{1,0:T(8,128)(2,1)S(1)}, bf16[512,128]{1,0:T(8,128)(2,1)}, u32[]{:S(2)}) copy-start(bf16[512,128]{1,0:T(8,128)(2,1)} %param.6) | copy-start | bytes 393220
  2.4 19.8 %all-to-all-start = ((bf16[32,24,128]{2,1,0:T(8,128)(2,1)}), bf16[32,24,128]{2,1,0:T(8,128)(2,1)S(1)}, u32[]{:S(2)}, u32[]{:S(2)}) async-start(bf16[32,24,128]{2,1,0:T(8,128)(2,1)} %pack_kernel.1), calls=%async_computation | async-start | bytes 393216 | tf_op jit(solution)/shard_map/all_to_all | solution.py:177
  12.7 3.6 %copy-start.1 = (f32[3,3,512]{2,1,0:T(4,128)S(1)}, f32[3,3,512]{2,1,0:T(4,128)}, u32[]{:S(2)}) copy-start(f32[3,3,512]{2,1,0:T(4,128)} %taps_ref.1) | copy-start | bytes 55300
  12.7 15.2 %collective-permute-start = (bf16[512,2]{1,0:T(8,128)(2,1)S(1)}, bf16[512,2]{1,0:T(8,128)(2,1)S(1)}, u32[]{:S(2)}, u32[]{:S(2)}) collective-permute-start(bf16[512,2]{1,0:T(8,128)(2,1)S(1)} %slice.33), channel_id=1, source_target_pairs={{0,8},{8,16},{16,24},{24,32},{32,40},{40,48},{48,56},{56,64},{64,7... | collective-permute-start | bytes 6152 | tf_op jit(solution)/shard_map/ppermute | solution.py:180
  16.3 0.7 %slice-start = ((f32[3,3,512]{2,1,0:T(4,128)}), f32[2,3,512]{2,1,0:T(4,128)S(1)}, s32[]{:S(2)}) async-start(f32[3,3,512]{2,1,0:T(4,128)} %taps_ref.1), calls=%async_computation.2 | async-start | bytes 32768 | tf_op jit(solution)/shard_map/slice | solution.py:183
  24.0 12.5 %all-to-all-start.1 = ((bf16[32,16,128]{2,1,0:T(8,128)(2,1)}), bf16[32,16,128]{2,1,0:T(8,128)(2,1)S(1)}, u32[]{:S(2)}, u32[]{:S(2)}) async-start(bf16[32,16,128]{2,1,0:T(8,128)(2,1)} %conv_kernel.1), calls=%async_computation.1 | async-start | bytes 262144 | tf_op jit(solution)/shard_map/all_to_all | solution.py:194

commit v3 on v2

v3 whole, which is shorter than its diff:
```python
import jax
import jax.numpy as jnp
from jax import lax
from jax.experimental import pallas as pl
from jax.experimental.pallas import tpu as pltpu
from jax.sharding import PartitionSpec as P

INTERPRET = False
LANES = 128
ROWS = 24
def ring_order(z0, x0, c0):
    return tuple(
        ((z + z0) % 4) * 8 + ((x + x0) % 4) * 2 + (c + c0) % 2
        for x in range(4)
        for z in range(4)
        for c in range(2)
    )


ORDER_IN = ring_order(2, 2, 1)
ORDER_OUT = ORDER_IN
F32 = jnp.float32
BF16 = jnp.bfloat16


def iota(shape, dim):
    return lax.broadcasted_iota(jnp.int32, shape, dim)


def one_hot(mask):
    return jnp.where(mask, 1.0, 0.0).astype(BF16)


def places(order):
    return [order.index(i) for i in range(len(order))]


def dot(a, b):
    return jnp.dot(a, b, preferred_element_type=F32)


def dot_t(a, b):
    return lax.dot_general(a, b, (((1,), (1,)), ((), ())), preferred_element_type=F32)


def pack_kernel(k_hbm, x_hbm, taps_hbm, lags_hbm, out_hbm, k_ref, x_ref, taps_ref, lags_ref, out_ref, sems):
    channels, length = k_ref.shape
    parts = lags_ref.shape[0]
    width = channels // parts
    block = length
    steps = channels // block
    peers = parts // steps
    copy = pltpu.make_async_copy
    loads = [
        copy(k_hbm, k_ref, sems.at[0]),
        copy(x_hbm, x_ref, sems.at[1]),
        copy(taps_hbm, taps_ref, sems.at[2]),
        copy(lags_hbm, lags_ref, sems.at[3]),
    ]
    for c in loads:
        c.start()

    src = iota((length, length), 0)
    dst = iota((length, length), 1)
    shifts = jnp.concatenate([one_hot(src == dst + i) for i in range(3)], axis=0)
    identity = one_hot(src == dst)
    hit = src == jnp.where(dst % 4 < 2, length - 2 + dst % 4, dst % 4 - 2)
    pick = jnp.concatenate([one_hot(hit & (dst % 8 < 4)), one_hot(hit & (dst % 8 >= 4))], axis=0)
    own = (dst // 8) == (src % width)
    tail = 8 * peers
    row = iota((tail, block), 0)
    gather = one_hot((row % 8 == 1) & (row // 8 == iota((tail, block), 1) // width))
    row = iota((tail, peers), 0)
    place = one_hot((row % 8 == 0) & (row // 8 == iota((tail, peers), 1)))

    for c in loads:
        c.wait()

    def short(moved, m, lanes):
        a, b, c = (taps_ref[m, i : i + 1, lanes] * moved[i * length : (i + 1) * length] for i in range(3))
        return a + b + c

    def gate(i):
        rows = slice(i * block, (i + 1) * block)
        k = k_ref[rows, :]
        x = x_ref[rows, :]
        edges = dot(jnp.concatenate([k, x], axis=1), pick)
        gated = short(dot_t(shifts, k), 1, rows) * short(dot_t(shifts, x), 2, rows)
        edges = jnp.where(own, edges, 0.0).astype(BF16)
        return jnp.where(src < 2, 0.0, gated).astype(BF16), edges

    def put(i, gated, edges):
        gated = dot_t(identity, gated).astype(BF16)
        rest = dot(gather, edges) + dot(place, lags_ref[i * peers : (i + 1) * peers, :])
        to = slice(i * peers, (i + 1) * peers)
        out_ref[to, 0:width, :] = gated.reshape(peers, width, length)
        out_ref[to, width : width + 8, :] = rest.astype(BF16).reshape(peers, 8, length)

    ahead = gate(0)
    for i in range(steps):
        current = ahead
        if i + 1 < steps:
            ahead = gate(i + 1)
        put(i, *current)
    store = copy(out_ref, out_hbm, sems.at[4])
    store.start()
    store.wait()


def conv_kernel(got_ref, weights_ref, skip_ref, out_ref):
    parts, _, length = got_ref.shape
    width = out_ref.shape[1]
    pairs = parts // 2
    at_stretch = places(ORDER_IN)

    tail = jnp.concatenate([got_ref[i, width : width + 8, :] for i in at_stretch], axis=0)
    row = iota((parts, 8 * parts), 0)
    col = iota((parts, 8 * parts), 1) - 1
    own = dot(one_hot(col == 8 * row), tail)
    last = dot(one_hot(col == 8 * row - 8), tail)
    lane = iota((parts, length), 1)
    joined = jnp.where(lane % 4 < 2, last, own)
    short = (
        weights_ref[0:1, :] * joined
        + weights_ref[1:2, :] * pltpu.roll(joined, 1, 1)
        + weights_ref[2:3, :] * pltpu.roll(joined, 2, 1)
    )
    first = short * pltpu.roll(short, length - 4, 1)
    lane = iota((width, length), 1)
    keep = (lane // 8 == iota((width, length), 0)) & (lane % 8 >= 2) & (lane % 8 < 4)
    src = iota((length, length), 0)
    dst = iota((length, length), 1)
    move = one_hot((src % 8 - 2 == dst) & (dst < 2))
    repeated = [jnp.where(keep, first[s : s + 1, :], 0.0).astype(BF16) for s in range(parts)]
    fixed = dot(jnp.concatenate(repeated, axis=0), move).astype(BF16)
    pieces = [got_ref[i, 0:width, :] + fixed[s * width : (s + 1) * width] for s, i in enumerate(at_stretch)]
    panel = jnp.concatenate(
        [jnp.concatenate(pieces[0::2], axis=0), jnp.concatenate(pieces[1::2], axis=0)], axis=1
    )

    upper = dst >= src

    def turn(b):
        taps = got_ref[at_stretch[b], width : width + 1, :].astype(F32)
        return pltpu.roll(jnp.broadcast_to(taps, (length, length)), 0, 1, stride=1, stride_axis=0)

    skip = jnp.concatenate([skip_ref[...]] * 2, axis=1)
    total = panel.astype(F32) * jnp.concatenate([skip] * pairs, axis=0)
    before = jnp.zeros((length, length), F32)
    left = jnp.zeros((length, length), BF16)
    for b in range(pairs):
        even, odd = turn(2 * b), turn(2 * b + 1)
        here = jnp.where(upper, even, before).astype(BF16)
        right = jnp.where(upper, odd, even).astype(BF16)
        block = jnp.concatenate(
            [jnp.concatenate([here, right], axis=1), jnp.concatenate([left, here], axis=1)], axis=0
        )
        before, left = odd, right
        live = (pairs - b) * width
        term = dot(panel[:live], block)
        if b:
            term = jnp.concatenate([jnp.zeros((b * width, 2 * length), F32), term], axis=0)
        total = total + term
    total = total.astype(BF16)
    for i, stretch in enumerate(ORDER_OUT):
        at = (stretch // 2) * width
        out_ref[i] = total[at : at + width, (stretch % 2) * length : (stretch % 2 + 1) * length]


def mix_kernel(back_ref, q_ref, out_ref):
    parts, width, length = back_ref.shape
    at_device = places(ORDER_OUT)
    for i, device in enumerate(ORDER_IN):
        rows = pl.ds(i * width, width)
        out_ref[rows, :] = (q_ref[rows, :] * back_ref[at_device[device]].astype(F32)).astype(BF16)


def call(kernel, out_shape, scratch=(), near=True):
    shape, dtype = out_shape
    out = pltpu.VMEM(shape, dtype) if near and not INTERPRET else jax.ShapeDtypeStruct(shape, dtype)
    return pl.pallas_call(
        kernel,
        out_shape=out,
        scratch_shapes=list(scratch),
        interpret=INTERPRET,
        name=kernel.__name__,
    )


def near(x):
    return x if INTERPRET else pltpu.with_memory_space_constraint(x, pltpu.VMEM)


def short_conv(stream, before, weights):
    joined = jnp.concatenate([before, stream], axis=1).astype(F32)
    length = stream.shape[1]
    return (
        weights[0][:, None] * joined[:, 2:]
        + weights[1][:, None] * joined[:, 1 : length + 1]
        + weights[2][:, None] * joined[:, 0:length]
    )


def exchange(chunks, order):
    return lax.all_to_all(
        chunks, "ctx", split_axis=0, concat_axis=0, tiled=True, axis_index_groups=[list(order)]
    )


def body(q_stream, k_stream, x_stream, short_taps, skip_gain, filter_taps):
    channels, length = q_stream.shape
    parts = lax.axis_size("ctx")
    width = channels // parts
    sent = pl.pallas_call(
        pack_kernel,
        out_shape=jax.ShapeDtypeStruct((parts, ROWS, length), BF16),
        in_specs=[pl.BlockSpec(memory_space=pl.ANY)] * 4,
        out_specs=pl.BlockSpec(memory_space=pl.ANY),
        scratch_shapes=[
            pltpu.VMEM((channels, length), BF16),
            pltpu.VMEM((channels, length), BF16),
            pltpu.VMEM(short_taps.shape, F32),
            pltpu.VMEM(filter_taps.shape, BF16),
            pltpu.VMEM((parts, ROWS, length), BF16),
            pltpu.SemaphoreType.DMA((5,)),
        ],
        interpret=INTERPRET,
        name="pack_kernel",
    )(k_stream, x_stream, short_taps, filter_taps)
    got = exchange(sent, ORDER_IN)

    pairs = [(i, i + 1) for i in range(parts - 1)]
    before = lax.ppermute(q_stream[:, -2:], "ctx", pairs)
    q_short = lax.optimization_barrier(short_conv(q_stream, before, short_taps[0]))
    first = jnp.asarray(places(ORDER_IN), jnp.int32)[lax.axis_index("ctx")] * width
    own = lax.dynamic_slice_in_dim(short_taps[1:], first, width, 2)
    own = jnp.repeat(jnp.transpose(own, (1, 2, 0)).reshape(3, 2 * width), 4, axis=1)
    weights = jnp.concatenate([own, jnp.zeros((5, length), F32)], axis=0)
    skip = lax.dynamic_slice_in_dim(skip_gain, first, width, 0)
    skip = jnp.broadcast_to(skip[:, None], (width, length))

    parted = call(
        conv_kernel,
        ((parts, width, length), BF16),
    )(near(got), near(weights), near(skip))
    back = exchange(parted, ORDER_OUT)
    return call(mix_kernel, ((channels, length), BF16), near=False)(near(back), near(q_short))


def solution(mesh):
    return jax.shard_map(
        body,
        mesh=mesh,
        in_specs=(
            P("ch", "ctx"),
            P("ch", "ctx"),
            P("ch", "ctx"),
            P(None, None, "ch"),
            P("ch"),
            P("ch", "ctx"),
        ),
        out_specs=P("ch", "ctx"),
        check_vma=False,
    )
```

time: 37.5 us -> 32.3 us (0.86)
  waiting for transfers between devices: 11.9 us -> 3.58 us
  starting transfers between devices: 17.6 us -> 19.7 us
  between operations: 0.11 us -> 0.8 us
  local copies, waits for them, and re-layouts: 2.08 us -> 2.62 us
    all_to_all x2, waiting for transfers between devices: 11.9 us -> 3.57 us  [exchange(): lax.all_to_all(chunks, 'ctx', split_axis=0, concat_axis=0, tiled=True, ax...]
    all_to_all x2, starting transfers between devices: 14.1 us -> 17.8 us  [exchange(): lax.all_to_all(chunks, 'ctx', split_axis=0, concat_axis=0, tiled=True, ax...]
    ppermute x1, starting transfers between devices: 3.54 us -> 1.93 us  [body(): before = lax.ppermute(q_stream[:, -2:], 'ctx', pairs)]
    slice x2, local copies, waits for them, and re-layouts: 0.69 us -> 0.01 us  [body(): own = lax.dynamic_slice_in_dim(short_taps[1:], first, width, 2)]
    unnamed x4 -> x6, local copies, waits for them, and re-layouts: 0.01 us -> 0.64 us
    dynamic_slice x0 -> x1, local copies, waits for them, and re-layouts: none -> 0.58 us  [body(): jnp.asarray(places(ORDER_IN), jnp.int32)[lax.axis_index('ctx')] * width]
  transfers between devices with their start and end apart: 3 -> 3, of which waited for: 2 -> 2; matrix products, arithmetic and copies ran while one was open for 5% -> 8% of each run, Pallas kernels for 5% -> 5%
where the time goes in v3:
time: 32.3 us; the launch traced here: 32 us
  starting transfers between devices  19.7 us (61%)
  Pallas kernels  4.71 us (15%)
  waiting for transfers between devices  3.58 us (11%)
  local copies, waits for them, and re-layouts  2.62 us (8%)
  between operations  0.8 us (2%)
  other arithmetic  0.55 us (2%)
    all_to_all x2, starting transfers between devices, exchange(): lax.all_to_all(chunks, 'ctx', split_axis=0, concat_axis=0, tiled=True, ax...  17.8 us
    all_to_all x2, waiting for transfers between devices, exchange(): lax.all_to_all(chunks, 'ctx', split_axis=0, concat_axis=0, tiled=True, ax...  3.57 us
    pallas_call x1, Pallas kernels, body(): pl.pallas_call(pack_kernel, out_shape=jax.ShapeDtypeStruct((parts, ROWS,...  2.47 us
    ppermute x1, starting transfers between devices, body(): before = lax.ppermute(q_stream[:, -2:], 'ctx', pairs)  1.93 us
    pallas_call x1, Pallas kernels, body(): call(conv_kernel, ((parts, width, length), BF16))  1.56 us
    dynamic_slice x1, local copies, waits for them, and re-layouts, body(): skip = lax.dynamic_slice_in_dim(skip_gain, first, width, 0)  0.76 us
    pallas_call x1, Pallas kernels, body(): call(mix_kernel, ((channels, length), BF16), near=False)  0.68 us
  transfers between devices with their start and end apart: 3, of which 2 were waited for; matrix products, arithmetic and copies ran while one was open for 8% of the time, Pallas kernels for 5%

profile of v3, /device:TPU:1, one launch (start us, length us, event | category | flops | bytes accessed | tf_op | source)
XLA Modules:
  0.0 32.0 jit_solution(4206678354252532601)
XLA Ops:
  0.0 2.5 %pack_kernel.1 = bf16[32,24,128]{2,1,0:T(8,128)(2,1)} custom-call(bf16[512,128]{1,0:T(8,128)(2,1)} %k_hbm.1, bf16[512,128]{1,0:T(8,128)(2,1)} %x_hbm.1, f32[3,3,512]{2,1,0:T(4,128)} %taps_hbm.1, bf16[32,128]{1,0:T(8,128)(2,1)} %lags_hbm.1), custom_call_target="tpu_custom_call" | custom-call | tf_op jit(solution)/shard_map/pack_kernel/pallas_call | solution.py:214
  2.5 0.0 copy-start
  2.5 10.7 %all-to-all-start = ((bf16[32,24,128]{2,1,0:T(8,128)(2,1)}), bf16[32,24,128]{2,1,0:T(8,128)(2,1)S(1)}, u32[]{:S(2)}, u32[]{:S(2)}) async-start(bf16[32,24,128]{2,1,0:T(8,128)(2,1)} %pack_kernel.1), calls=%async_computation | async-start | bytes 393216 | tf_op jit(solution)/shard_map/all_to_all | solution.py:205
  13.2 0.1 slice.33
  13.3 1.9 %collective-permute-start = (bf16[512,2]{1,0:T(8,128)(2,1)S(1)}, bf16[512,2]{1,0:T(8,128)(2,1)S(1)}, u32[]{:S(2)}, u32[]{:S(2)}) collective-permute-start(bf16[512,2]{1,0:T(8,128)(2,1)S(1)} %slice.33), channel_id=1, source_target_pairs={{0,8},{8,16},{16,24},{24,32},{32,40},{40,48},{48,56},{56,64},{64,7... | collective-permute-start | bytes 6152 | tf_op jit(solution)/shard_map/ppermute | solution.py:233
  15.2 0.0 copy-start.2
  15.3 0.0 copy-start.1
  15.3 0.0 slice-start
  15.3 0.6 %copy-done.2 = s32[32]{0:T(128)S(1)} copy-done((s32[32]{0:T(128)S(1)}, s32[32]{0:T(128)}, u32[]{:S(2)}) %copy-start.2) | copy-done | bytes 152
  15.9 0.6 %dynamic_slice.9 = s32[1]{0:T(128)} dynamic-slice(s32[32]{0:T(128)S(1)} %copy-done.2, s32[]{:T(128)S(6)} %select_n.7), dynamic_slice_sizes={1} | dynamic-slice | bytes 12 | tf_op jit(solution)/shard_map/dynamic_slice | solution.py:235
  17.2 0.1 dynamic-slice_bitcast_fusion
  17.3 0.8 %dynamic_slice.11 = f32[16]{0:T(128)S(1)} dynamic-slice(f32[512]{0:T(512)} %param.11, s32[]{:T(128)S(6)} %select_n.8), dynamic_slice_sizes={16} | dynamic-slice | bytes 132 | tf_op jit(solution)/shard_map/dynamic_slice | solution.py:239
  18.0 0.1 copy.9
  18.1 0.1 reshape.18
  18.2 0.1 broadcast_in_dim.4
  18.3 0.1 reshape.19
  18.4 0.3 all-to-all-done.got_ref
  18.7 0.1 broadcast_in_dim.5.skip_ref
  18.8 1.6 %conv_kernel.1 = bf16[32,16,128]{2,1,0:T(8,128)(2,1)} custom-call(bf16[32,24,128]{2,1,0:T(8,128)(2,1)S(1)} %all-to-all-done.got_ref, f32[8,128]{1,0:T(8,128)S(1)} %concatenate.6.weights_ref, f32[16,128]{1,0:T(8,128)S(1)} %broadcast_in_dim.5.skip_ref), custom_call_target="tpu_custom_call" | custom-call | tf_op jit(solution)/shard_map/conv_kernel/pallas_call | solution.py:242
  20.3 7.1 %all-to-all-start.1 = ((bf16[32,16,128]{2,1,0:T(8,128)(2,1)}), bf16[32,16,128]{2,1,0:T(8,128)(2,1)S(1)}, u32[]{:S(2)}, u32[]{:S(2)}) async-start(bf16[32,16,128]{2,1,0:T(8,128)(2,1)} %conv_kernel.1), calls=%async_computation.1 | async-start | bytes 262144 | tf_op jit(solution)/shard_map/all_to_all | solution.py:205
  27.5 0.1 maximum_convert_fusion
  27.6 0.4 %fusion.q_ref = f32[512,128]{1,0:T(8,128)S(1)} fusion(f32[512,130]{1,0:T(8,128)S(1)} %maximum_convert_fusion, f32[512]{0:T(512)S(1)} %bitcast.7, f32[512]{0:T(512)S(1)} %bitcast.8, f32[512]{0:T(512)S(1)} %bitcast.6), kind=kLoop, calls=%fused_computation.1 | loop fusion | flops 327680 | bytes 1054720 | tf_op jit(solution)/shard_map/add | solution.py:198
  28.0 3.3 %all-to-all-done.1.back_ref = bf16[32,16,128]{2,1,0:T(8,128)(2,1)S(1)} async-done(((bf16[32,16,128]{2,1,0:T(8,128)(2,1)}), bf16[32,16,128]{2,1,0:T(8,128)(2,1)S(1)}, u32[]{:S(2)}, u32[]{:S(2)}) %all-to-all-start.1) | async-done | bytes 131104 | tf_op jit(solution)/shard_map/all_to_all | solution.py:205
  31.3 0.7 %mix_kernel.1 = bf16[512,128]{1,0:T(8,128)(2,1)} custom-call(bf16[32,16,128]{2,1,0:T(8,128)(2,1)S(1)} %all-to-all-done.1.back_ref, f32[512,128]{1,0:T(8,128)S(1)} %fusion.q_ref), custom_call_target="tpu_custom_call" | custom-call | tf_op jit(solution)/shard_map/mix_kernel/pallas_call | solution.py:247
  (6 shorter events, 0.0 us)
Async XLA Ops:
  2.5 10.7 %copy-start = (bf16[512,128]{1,0:T(8,128)(2,1)S(1)}, bf16[512,128]{1,0:T(8,128)(2,1)}, u32[]{:S(2)}) copy-start(bf16[512,128]{1,0:T(8,128)(2,1)} %param.7) | copy-start | bytes 393220
  2.5 16.2 %all-to-all-start = ((bf16[32,24,128]{2,1,0:T(8,128)(2,1)}), bf16[32,24,128]{2,1,0:T(8,128)(2,1)S(1)}, u32[]{:S(2)}, u32[]{:S(2)}) async-start(bf16[32,24,128]{2,1,0:T(8,128)(2,1)} %pack_kernel.1), calls=%async_computation | async-start | bytes 393216 | tf_op jit(solution)/shard_map/all_to_all | solution.py:205
  13.3 14.2 %collective-permute-start = (bf16[512,2]{1,0:T(8,128)(2,1)S(1)}, bf16[512,2]{1,0:T(8,128)(2,1)S(1)}, u32[]{:S(2)}, u32[]{:S(2)}) collective-permute-start(bf16[512,2]{1,0:T(8,128)(2,1)S(1)} %slice.33), channel_id=1, source_target_pairs={{0,8},{8,16},{16,24},{24,32},{32,40},{40,48},{48,56},{56,64},{64,7... | collective-permute-start | bytes 6152 | tf_op jit(solution)/shard_map/ppermute | solution.py:233
  15.2 0.7 %copy-start.2 = (s32[32]{0:T(128)S(1)}, s32[32]{0:T(128)}, u32[]{:S(2)}) copy-start(s32[32]{0:T(128)} %constant.19.clone) | copy-start | bytes 388
  15.3 1.9 %copy-start.1 = (f32[3,3,512]{2,1,0:T(4,128)S(1)}, f32[3,3,512]{2,1,0:T(4,128)}, u32[]{:S(2)}) copy-start(f32[3,3,512]{2,1,0:T(4,128)} %taps_hbm.1) | copy-start | bytes 55300
  15.3 1.9 %slice-start = ((f32[3,3,512]{2,1,0:T(4,128)}), f32[2,3,512]{2,1,0:T(4,128)S(1)}, s32[]{:S(2)}) async-start(f32[3,3,512]{2,1,0:T(4,128)} %taps_hbm.1), calls=%async_computation.2 | async-start | bytes 32768 | tf_op jit(solution)/shard_map/slice | solution.py:236
  20.3 11.0 %all-to-all-start.1 = ((bf16[32,16,128]{2,1,0:T(8,128)(2,1)}), bf16[32,16,128]{2,1,0:T(8,128)(2,1)S(1)}, u32[]{:S(2)}, u32[]{:S(2)}) async-start(bf16[32,16,128]{2,1,0:T(8,128)(2,1)} %conv_kernel.1), calls=%async_computation.1 | async-start | bytes 262144 | tf_op jit(solution)/shard_map/all_to_all | solution.py:205

commit v4 on v3

--- a/solution.py
+++ b/solution.py
@@ -7,7 +7,7 @@
 
 INTERPRET = False
 LANES = 128
-ROWS = 24
+EXTRA = 2
 def ring_order(z0, x0, c0):
     return tuple(
         ((z + z0) % 4) * 8 + ((x + x0) % 4) * 2 + (c + c0) % 2
@@ -19,6 +19,12 @@
 
 ORDER_IN = ring_order(2, 2, 1)
 ORDER_OUT = ORDER_IN
+
+
+def slot_of(i):
+    return ((i // 2 + 2) % 4) * 8 + ((i // 8 + 2) % 4) * 2 + (i + 1) % 2
+
+
 F32 = jnp.float32
 BF16 = jnp.bfloat16
 
@@ -43,7 +49,10 @@
     return lax.dot_general(a, b, (((1,), (1,)), ((), ())), preferred_element_type=F32)
 
 
-def pack_kernel(k_hbm, x_hbm, taps_hbm, lags_hbm, out_hbm, k_ref, x_ref, taps_ref, lags_ref, out_ref, sems):
+def pack_kernel(
+    k_hbm, x_hbm, taps_hbm, lags_hbm, gain_hbm, out_hbm, weights_ref, skip_ref,
+    k_ref, x_ref, taps_ref, lags_ref, gain_ref, out_ref, sems,
+):
     channels, length = k_ref.shape
     parts = lags_ref.shape[0]
     width = channels // parts
@@ -51,27 +60,25 @@
     steps = channels // block
     peers = parts // steps
     copy = pltpu.make_async_copy
-    loads = [
-        copy(k_hbm, k_ref, sems.at[0]),
-        copy(x_hbm, x_ref, sems.at[1]),
-        copy(taps_hbm, taps_ref, sems.at[2]),
-        copy(lags_hbm, lags_ref, sems.at[3]),
-    ]
+    pairs = [(k_hbm, k_ref), (x_hbm, x_ref), (taps_hbm, taps_ref), (lags_hbm, lags_ref), (gain_hbm, gain_ref)]
+    loads = [copy(a, b, sems.at[i]) for i, (a, b) in enumerate(pairs)]
     for c in loads:
         c.start()
 
     src = iota((length, length), 0)
     dst = iota((length, length), 1)
     shifts = jnp.concatenate([one_hot(src == dst + i) for i in range(3)], axis=0)
-    identity = one_hot(src == dst)
-    hit = src == jnp.where(dst % 4 < 2, length - 2 + dst % 4, dst % 4 - 2)
-    pick = jnp.concatenate([one_hot(hit & (dst % 8 < 4)), one_hot(hit & (dst % 8 >= 4))], axis=0)
-    own = (dst // 8) == (src % width)
-    tail = 8 * peers
-    row = iota((tail, block), 0)
-    gather = one_hot((row % 8 == 1) & (row // 8 == iota((tail, block), 1) // width))
-    row = iota((tail, peers), 0)
-    place = one_hot((row % 8 == 0) & (row // 8 == iota((tail, peers), 1)))
+    kind = (dst + 2) % 8
+    hit = src == jnp.where(kind % 4 < 2, length - 2 + kind % 4, kind % 4 - 2)
+    pick = jnp.concatenate([one_hot(hit & (kind < 4)), one_hot(hit & (kind >= 4))], axis=0)
+    own = (dst + 2 + 8 * src) % length < 8
+    stride = width + EXTRA
+    row = iota((peers * stride, block), 0)
+    col = iota((peers * stride, block), 1)
+    place = one_hot((row // stride == col // width) & (row % stride == col % width))
+    gather = one_hot((row // stride == col // width) & (row % stride == width + 1))
+    row = iota((peers * stride, peers), 0)
+    spare = one_hot(row == iota((peers * stride, peers), 1) * stride + width)
 
     for c in loads:
         c.wait()
@@ -90,62 +97,76 @@
         return jnp.where(src < 2, 0.0, gated).astype(BF16), edges
 
     def put(i, gated, edges):
-        gated = dot_t(identity, gated).astype(BF16)
-        rest = dot(gather, edges) + dot(place, lags_ref[i * peers : (i + 1) * peers, :])
-        to = slice(i * peers, (i + 1) * peers)
-        out_ref[to, 0:width, :] = gated.reshape(peers, width, length)
-        out_ref[to, width : width + 8, :] = rest.astype(BF16).reshape(peers, 8, length)
-
+        chunks = dot_t(place, gated) + dot(gather, edges) + dot(spare, lags_ref[i * peers : (i + 1) * peers, :])
+        out_ref[i * peers * stride : (i + 1) * peers * stride, :] = chunks.astype(BF16)
+
+    stores = []
     ahead = gate(0)
     for i in range(steps):
         current = ahead
         if i + 1 < steps:
             ahead = gate(i + 1)
         put(i, *current)
-    store = copy(out_ref, out_hbm, sems.at[4])
-    store.start()
-    store.wait()
+        to = pl.ds(i * peers * stride, peers * stride)
+        stores.append(copy(out_ref.at[to], out_hbm.at[to], sems.at[5 + i]))
+        stores[-1].start()
+
+    rows = jnp.concatenate([taps_ref[1], taps_ref[2], gain_ref[...], jnp.zeros((1, channels), F32)], axis=0)
+    rows = pltpu.roll(rows, (channels - slot_of(lax.axis_index("ctx")) * width) % channels, 1)[:, :length]
+    columns = rows.T[:width]
+    lane = iota((width, length), 1)
+    mine = (lane + 2 + 8 * iota((width, length), 0)) % length < 8
+    parted = []
+    for j in range(3):
+        both = jnp.where((lane + 2) % 8 < 4, columns[:, j : j + 1], columns[:, 3 + j : 4 + j])
+        parted.append(jnp.sum(jnp.where(mine, both, 0.0), axis=0, keepdims=True))
+    weights_ref[...] = jnp.concatenate(parted + [jnp.zeros((5, length), F32)], axis=0)
+    skip_ref[...] = jnp.broadcast_to(columns[:, 6:7], (width, length))
+    for c in stores:
+        c.wait()
 
 
 def conv_kernel(got_ref, weights_ref, skip_ref, out_ref):
-    parts, _, length = got_ref.shape
-    width = out_ref.shape[1]
+    parts, width, length = out_ref.shape
     pairs = parts // 2
+    stride = width + EXTRA
     at_stretch = places(ORDER_IN)
 
-    tail = jnp.concatenate([got_ref[i, width : width + 8, :] for i in at_stretch], axis=0)
-    row = iota((parts, 8 * parts), 0)
-    col = iota((parts, 8 * parts), 1) - 1
-    own = dot(one_hot(col == 8 * row), tail)
-    last = dot(one_hot(col == 8 * row - 8), tail)
     lane = iota((parts, length), 1)
-    joined = jnp.where(lane % 4 < 2, last, own)
+    at = [i * stride + width + 1 for i in at_stretch]
+    own = jnp.concatenate([got_ref[i : i + 1, :].astype(F32) for i in at], axis=0)
+    last = jnp.concatenate([jnp.zeros((1, length), F32), own[: parts - 1]], axis=0)
+    joined = jnp.where((lane + 2) % 4 < 2, last, own)
     short = (
         weights_ref[0:1, :] * joined
         + weights_ref[1:2, :] * pltpu.roll(joined, 1, 1)
         + weights_ref[2:3, :] * pltpu.roll(joined, 2, 1)
     )
     first = short * pltpu.roll(short, length - 4, 1)
-    lane = iota((width, length), 1)
-    keep = (lane // 8 == iota((width, length), 0)) & (lane % 8 >= 2) & (lane % 8 < 4)
     src = iota((length, length), 0)
     dst = iota((length, length), 1)
-    move = one_hot((src % 8 - 2 == dst) & (dst < 2))
-    repeated = [jnp.where(keep, first[s : s + 1, :], 0.0).astype(BF16) for s in range(parts)]
-    fixed = dot(jnp.concatenate(repeated, axis=0), move).astype(BF16)
-    pieces = [got_ref[i, 0:width, :] + fixed[s * width : (s + 1) * width] for s, i in enumerate(at_stretch)]
-    panel = jnp.concatenate(
+    head = iota((width, length), 1) < 2
+
+    def fixed(s):
+        rows = jnp.broadcast_to(first[s : s + 1, :], (width, length))
+        rows = pltpu.roll(rows, 0, 1, stride=8, stride_axis=0)
+        return jnp.where(head, rows, got_ref[at_stretch[s] * stride : at_stretch[s] * stride + width, :].astype(F32))
+
+    pieces = [fixed(s) for s in range(parts)]
+    wide = jnp.concatenate(
         [jnp.concatenate(pieces[0::2], axis=0), jnp.concatenate(pieces[1::2], axis=0)], axis=1
     )
+    panel = wide.astype(BF16)
+    wide = panel.astype(F32)
 
     upper = dst >= src
 
     def turn(b):
-        taps = got_ref[at_stretch[b], width : width + 1, :].astype(F32)
+        taps = got_ref[at_stretch[b] * stride + width : at_stretch[b] * stride + width + 1, :].astype(F32)
         return pltpu.roll(jnp.broadcast_to(taps, (length, length)), 0, 1, stride=1, stride_axis=0)
 
     skip = jnp.concatenate([skip_ref[...]] * 2, axis=1)
-    total = panel.astype(F32) * jnp.concatenate([skip] * pairs, axis=0)
+    total = wide * jnp.concatenate([skip] * pairs, axis=0)
     before = jnp.zeros((length, length), F32)
     left = jnp.zeros((length, length), BF16)
     for b in range(pairs):
@@ -211,33 +232,37 @@
     channels, length = q_stream.shape
     parts = lax.axis_size("ctx")
     width = channels // parts
-    sent = pl.pallas_call(
+    near_shape = jax.ShapeDtypeStruct if INTERPRET else pltpu.VMEM
+    sent, weights, skip = pl.pallas_call(
         pack_kernel,
-        out_shape=jax.ShapeDtypeStruct((parts, ROWS, length), BF16),
-        in_specs=[pl.BlockSpec(memory_space=pl.ANY)] * 4,
-        out_specs=pl.BlockSpec(memory_space=pl.ANY),
+        out_shape=(
+            jax.ShapeDtypeStruct((parts * (width + EXTRA), length), BF16),
+            near_shape((8, length), F32),
+            near_shape((width, length), F32),
+        ),
+        in_specs=[pl.BlockSpec(memory_space=pl.ANY)] * 5,
+        out_specs=(
+            pl.BlockSpec(memory_space=pl.ANY),
+            pl.BlockSpec(memory_space=pltpu.VMEM),
+            pl.BlockSpec(memory_space=pltpu.VMEM),
+        ),
         scratch_shapes=[
             pltpu.VMEM((channels, length), BF16),
             pltpu.VMEM((channels, length), BF16),
             pltpu.VMEM(short_taps.shape, F32),
             pltpu.VMEM(filter_taps.shape, BF16),
-            pltpu.VMEM((parts, ROWS, length), BF16),
-            pltpu.SemaphoreType.DMA((5,)),
+            pltpu.VMEM((1, channels), F32),
+            pltpu.VMEM((parts * (width + EXTRA), length), BF16),
+            pltpu.SemaphoreType.DMA((5 + channels // length,)),
         ],
         interpret=INTERPRET,
         name="pack_kernel",
-    )(k_stream, x_stream, short_taps, filter_taps)
-    got = exchange(sent, ORDER_IN)
+    )(k_stream, x_stream, short_taps, filter_taps, skip_gain[None, :])
+    got = exchange(sent.reshape(parts, (width + EXTRA) // 2, 2, length), ORDER_IN).reshape(sent.shape)
 
     pairs = [(i, i + 1) for i in range(parts - 1)]
     before = lax.ppermute(q_stream[:, -2:], "ctx", pairs)
     q_short = lax.optimization_barrier(short_conv(q_stream, before, short_taps[0]))
-    first = jnp.asarray(places(ORDER_IN), jnp.int32)[lax.axis_index("ctx")] * width
-    own = lax.dynamic_slice_in_dim(short_taps[1:], first, width, 2)
-    own = jnp.repeat(jnp.transpose(own, (1, 2, 0)).reshape(3, 2 * width), 4, axis=1)
-    weights = jnp.concatenate([own, jnp.zeros((5, length), F32)], axis=0)
-    skip = lax.dynamic_slice_in_dim(skip_gain, first, width, 0)
-    skip = jnp.broadcast_to(skip[:, None], (width, length))
 
     parted = call(
         conv_kernel,

time: 32.3 us -> 31.4 us (0.972)
  local copies, waits for them, and re-layouts: 2.62 us -> 0.92 us
  waiting for transfers between devices: 3.58 us -> 5.02 us
  between operations: 0.8 us -> 0.08 us
    all_to_all x2, waiting for transfers between devices: 3.57 us -> 5.01 us  [exchange(): lax.all_to_all(chunks, 'ctx', split_axis=0, concat_axis=0, tiled=True, ax...]
    dynamic_slice x2 -> x0, local copies, waits for them, and re-layouts: 1.34 us -> none  [the longest x1 0.76 us: body(): skip = lax.dynamic_slice_in_dim(skip_gain, first, width, 0)]
    slice x1, local copies, waits for them, and re-layouts: 0.01 us -> 0.82 us  [short_conv(): weights[0][:, None] * joined[:, 2:]]
    unnamed x6 -> x2, local copies, waits for them, and re-layouts: 0.64 us -> 0.01 us
  transfers between devices with their start and end apart: 3 -> 3, of which waited for: 2 -> 2; matrix products, arithmetic and copies ran while one was open for 8% -> 5% of each run, Pallas kernels for 5% -> 4%
where the time goes in v4:
time: 31.4 us; the launch traced here: 31 us
  starting transfers between devices  19.9 us (63%)
  waiting for transfers between devices  5.02 us (16%)
  Pallas kernels  4.57 us (15%)
  local copies, waits for them, and re-layouts  0.92 us (3%)
  other arithmetic  0.55 us (2%)
    all_to_all x2, starting transfers between devices, exchange(): lax.all_to_all(chunks, 'ctx', split_axis=0, concat_axis=0, tiled=True, ax...  18 us
    all_to_all x2, waiting for transfers between devices, exchange(): lax.all_to_all(chunks, 'ctx', split_axis=0, concat_axis=0, tiled=True, ax...  5.01 us
    pallas_call x1, Pallas kernels, body(): pl.pallas_call(pack_kernel, out_shape=(jax.ShapeDtypeStruct((parts * (wid...  2.51 us
    ppermute x1, starting transfers between devices, body(): before = lax.ppermute(q_stream[:, -2:], 'ctx', pairs)  1.93 us
    pallas_call x1, Pallas kernels, body(): call(conv_kernel, ((parts, width, length), BF16))  1.38 us
    slice x1, local copies, waits for them, and re-layouts, short_conv(): weights[0][:, None] * joined[:, 2:]  0.82 us
    pallas_call x1, Pallas kernels, body(): call(mix_kernel, ((channels, length), BF16), near=False)  0.68 us
  transfers between devices with their start and end apart: 3, of which 2 were waited for; matrix products, arithmetic and copies ran while one was open for 5% of the time, Pallas kernels for 4%

profile of v4, /device:TPU:1, one launch (start us, length us, event | category | flops | bytes accessed | tf_op | source)
XLA Modules:
  0.0 31.0 jit_solution(453146623621386500)
XLA Ops:
  0.0 2.5 %pack_kernel.1 = (bf16[576,128]{1,0:T(8,128)(2,1)}, f32[8,128]{1,0:T(8,128)S(1)}, f32[16,128]{1,0:T(8,128)S(1)}) custom-call(bf16[512,128]{1,0:T(8,128)(2,1)} %k_hbm.1, bf16[512,128]{1,0:T(8,128)(2,1)} %x_hbm.1, f32[3,3,512]{2,1,0:T(4,128)} %taps_hbm.1, bf16[32,128]{1,0:T(8,128)(2,1)} %lags_hbm.1, f32[1,512]{1,0:T(1,128)} %bitcast.11), custom_call_target="tpu_custom_call" | custom-call | tf_op jit(solution)/shard_map/pack_kernel/pallas_call | solution.py:236
  2.5 0.0 copy-start
  2.5 10.7 %all-to-all-start = ((bf16[32,9,2,128]{3,2,1,0:T(2,128)(2,1)}), bf16[32,9,2,128]{3,2,1,0:T(2,128)(2,1)S(1)}, u32[]{:S(2)}, u32[]{:S(2)}) async-start(bf16[32,9,2,128]{3,2,1,0:T(2,128)(2,1)} %bitcast.7), calls=%async_computation | async-start | bytes 294912 | tf_op jit(solution)/shard_map/all_to_all | solution.py:226
  13.2 0.0 copy-done
  13.2 0.1 slice.29
  13.3 1.9 %collective-permute-start = (bf16[512,2]{1,0:T(8,128)(2,1)S(1)}, bf16[512,2]{1,0:T(8,128)(2,1)S(1)}, u32[]{:S(2)}, u32[]{:S(2)}) collective-permute-start(bf16[512,2]{1,0:T(8,128)(2,1)S(1)} %slice.29), channel_id=1, source_target_pairs={{0,8},{8,16},{16,24},{24,32},{32,40},{40,48},{48,56},{56,64},{64,7... | collective-permute-start | bytes 6152 | tf_op jit(solution)/shard_map/ppermute | solution.py:264
  15.3 0.8 %fusion.2 = (f32[1,1,512]{2,1,0:T(1,128)S(1)}, f32[1,1,512]{2,1,0:T(1,128)S(1)}, f32[1,1,512]{2,1,0:T(1,128)S(1)}) fusion(f32[3,3,512]{2,1,0:T(4,128)} %taps_hbm.1), kind=kLoop, calls=%fused_computation.6 | loop fusion | bytes 12288 | tf_op jit(solution)/shard_map/slice | solution.py:219
  16.1 1.8 %all-to-all-done = bf16[32,9,2,128]{3,2,1,0:T(2,128)(2,1)S(1)} async-done(((bf16[32,9,2,128]{3,2,1,0:T(2,128)(2,1)}), bf16[32,9,2,128]{3,2,1,0:T(2,128)(2,1)S(1)}, u32[]{:S(2)}, u32[]{:S(2)}) %all-to-all-start) | async-done | bytes 147488 | tf_op jit(solution)/shard_map/all_to_all | solution.py:226
  17.9 1.4 %conv_kernel.1 = bf16[32,16,128]{2,1,0:T(8,128)(2,1)} custom-call(bf16[576,128]{1,0:T(8,128)(2,1)S(1)} %bitcast.6, f32[8,128]{1,0:T(8,128)S(1)} %get-tuple-element.9.weights_ref, f32[16,128]{1,0:T(8,128)S(1)} %get-tuple-element.10.skip_ref), custom_call_target="tpu_custom_call" | custom-call | tf_op jit(solution)/shard_map/conv_kernel/pallas_call | solution.py:267
  19.2 7.3 %all-to-all-start.1 = ((bf16[32,16,128]{2,1,0:T(8,128)(2,1)}), bf16[32,16,128]{2,1,0:T(8,128)(2,1)S(1)}, u32[]{:S(2)}, u32[]{:S(2)}) async-start(bf16[32,16,128]{2,1,0:T(8,128)(2,1)} %conv_kernel.1), calls=%async_computation.1 | async-start | bytes 262144 | tf_op jit(solution)/shard_map/all_to_all | solution.py:226
  26.5 0.0 collective-permute-done
  26.5 0.1 maximum_convert_fusion
  26.7 0.4 %fusion.q_ref = f32[512,128]{1,0:T(8,128)S(1)} fusion(f32[512,130]{1,0:T(8,128)S(1)} %maximum_convert_fusion, f32[512]{0:T(512)S(1)} %bitcast.9, f32[512]{0:T(512)S(1)} %bitcast.10, f32[512]{0:T(512)S(1)} %bitcast.8), kind=kLoop, calls=%fused_computation.1 | loop fusion | flops 327680 | bytes 1054720 | tf_op jit(solution)/shard_map/add | solution.py:219
  27.1 3.3 %all-to-all-done.1.back_ref = bf16[32,16,128]{2,1,0:T(8,128)(2,1)S(1)} async-done(((bf16[32,16,128]{2,1,0:T(8,128)(2,1)}), bf16[32,16,128]{2,1,0:T(8,128)(2,1)S(1)}, u32[]{:S(2)}, u32[]{:S(2)}) %all-to-all-start.1) | async-done | bytes 131104 | tf_op jit(solution)/shard_map/all_to_all | solution.py:226
  30.3 0.7 %mix_kernel.1 = bf16[512,128]{1,0:T(8,128)(2,1)} custom-call(bf16[32,16,128]{2,1,0:T(8,128)(2,1)S(1)} %all-to-all-done.1.back_ref, f32[512,128]{1,0:T(8,128)S(1)} %fusion.q_ref), custom_call_target="tpu_custom_call" | custom-call | tf_op jit(solution)/shard_map/mix_kernel/pallas_call | solution.py:272
Async XLA Ops:
  2.5 10.7 %copy-start = (bf16[512,128]{1,0:T(8,128)(2,1)S(1)}, bf16[512,128]{1,0:T(8,128)(2,1)}, u32[]{:S(2)}) copy-start(bf16[512,128]{1,0:T(8,128)(2,1)} %param.6) | copy-start | bytes 393220
  2.5 15.3 %all-to-all-start = ((bf16[32,9,2,128]{3,2,1,0:T(2,128)(2,1)}), bf16[32,9,2,128]{3,2,1,0:T(2,128)(2,1)S(1)}, u32[]{:S(2)}, u32[]{:S(2)}) async-start(bf16[32,9,2,128]{3,2,1,0:T(2,128)(2,1)} %bitcast.7), calls=%async_computation | async-start | bytes 294912 | tf_op jit(solution)/shard_map/all_to_all | solution.py:226
  13.3 13.2 %collective-permute-start = (bf16[512,2]{1,0:T(8,128)(2,1)S(1)}, bf16[512,2]{1,0:T(8,128)(2,1)S(1)}, u32[]{:S(2)}, u32[]{:S(2)}) collective-permute-start(bf16[512,2]{1,0:T(8,128)(2,1)S(1)} %slice.29), channel_id=1, source_target_pairs={{0,8},{8,16},{16,24},{24,32},{32,40},{40,48},{48,56},{56,64},{64,7... | collective-permute-start | bytes 6152 | tf_op jit(solution)/shard_map/ppermute | solution.py:264
  19.2 11.1 %all-to-all-start.1 = ((bf16[32,16,128]{2,1,0:T(8,128)(2,1)}), bf16[32,16,128]{2,1,0:T(8,128)(2,1)S(1)}, u32[]{:S(2)}, u32[]{:S(2)}) async-start(bf16[32,16,128]{2,1,0:T(8,128)(2,1)} %conv_kernel.1), calls=%async_computation.1 | async-start | bytes 262144 | tf_op jit(solution)/shard_map/all_to_all | solution.py:226

commit v5 on v4

--- a/solution.py
+++ b/solution.py
@@ -7,6 +7,7 @@
 
 INTERPRET = False
 LANES = 128
+FLUSH = 8
 EXTRA = 2
 def ring_order(z0, x0, c0):
     return tuple(
@@ -51,7 +52,7 @@
 
 def pack_kernel(
     k_hbm, x_hbm, taps_hbm, lags_hbm, gain_hbm, out_hbm, weights_ref, skip_ref,
-    k_ref, x_ref, taps_ref, lags_ref, gain_ref, out_ref, sems,
+    k_ref, x_ref, taps_ref, lags_ref, gain_ref, out_ref, shifts, pick, own, place, gather, sems,
 ):
     channels, length = k_ref.shape
     parts = lags_ref.shape[0]
@@ -67,47 +68,63 @@
 
     src = iota((length, length), 0)
     dst = iota((length, length), 1)
-    shifts = jnp.concatenate([one_hot(src == dst + i) for i in range(3)], axis=0)
-    kind = (dst + 2) % 8
-    hit = src == jnp.where(kind % 4 < 2, length - 2 + kind % 4, kind % 4 - 2)
-    pick = jnp.concatenate([one_hot(hit & (kind < 4)), one_hot(hit & (kind >= 4))], axis=0)
-    own = (dst + 2 + 8 * src) % length < 8
+    for i in range(3):
+        shifts[i * length : (i + 1) * length, :] = one_hot(src == dst + i)
+    kind = (dst + 2) & 7
+    hit = src == (((kind & 3) + length - 2) & (length - 1))
+    pick[0:length, :] = one_hot(hit & (kind < 4))
+    pick[length:, :] = one_hot(hit & (kind >= 4))
+    own[...] = one_hot(((dst + 2 + 8 * src) & (length - 1)) < 8)
     stride = width + EXTRA
     row = iota((peers * stride, block), 0)
     col = iota((peers * stride, block), 1)
-    place = one_hot((row // stride == col // width) & (row % stride == col % width))
-    gather = one_hot((row // stride == col // width) & (row % stride == width + 1))
-    row = iota((peers * stride, peers), 0)
-    spare = one_hot(row == iota((peers * stride, peers), 1) * stride + width)
+    peer = col // width
+    place[...] = one_hot(row == col + EXTRA * peer)
+    row = iota(gather.shape, 0)
+    col = iota(gather.shape, 1)
+    sample = (col < block) & (row == stride * (col // width) + width + 1)
+    lag = (col >= block) & (col < block + peers) & (row == stride * (col - block) + width)
+    gather[...] = one_hot(sample | lag)
 
     for c in loads:
         c.wait()
 
-    def short(moved, m, lanes):
-        a, b, c = (taps_ref[m, i : i + 1, lanes] * moved[i * length : (i + 1) * length] for i in range(3))
+    def short(moved, m, i, at):
+        lanes = slice(i * block, (i + 1) * block)
+        a, b, c = (
+            taps_ref[m, j : j + 1, lanes] * moved[j * length : (j + 1) * length, at * block : (at + 1) * block]
+            for j in range(3)
+        )
         return a + b + c
 
     def gate(i):
-        rows = slice(i * block, (i + 1) * block)
+        rows = slice(i * block, (i + 2) * block)
         k = k_ref[rows, :]
         x = x_ref[rows, :]
-        edges = dot(jnp.concatenate([k, x], axis=1), pick)
-        gated = short(dot_t(shifts, k), 1, rows) * short(dot_t(shifts, x), 2, rows)
-        edges = jnp.where(own, edges, 0.0).astype(BF16)
-        return jnp.where(src < 2, 0.0, gated).astype(BF16), edges
+        moved_k = dot_t(shifts[...], k)
+        moved_x = dot_t(shifts[...], x)
+        edges = dot(jnp.concatenate([k, x], axis=1), pick[...]).astype(BF16)
+        gated = [short(moved_k, 1, i + j, j) * short(moved_x, 2, i + j, j) for j in range(2)]
+        return jnp.concatenate(gated, axis=0).astype(BF16), edges
 
     def put(i, gated, edges):
-        chunks = dot_t(place, gated) + dot(gather, edges) + dot(spare, lags_ref[i * peers : (i + 1) * peers, :])
-        out_ref[i * peers * stride : (i + 1) * peers * stride, :] = chunks.astype(BF16)
+        masked = jnp.concatenate([edges[:block] * own[...], edges[block:] * own[...]], axis=1)
+        lags = lags_ref[i * peers : (i + 2) * peers, :].astype(F32)
+        lags = jnp.concatenate([lags, jnp.concatenate([lags[peers:], lags[:peers]], axis=0)], axis=1)
+        rest = jnp.concatenate([masked, lags.astype(BF16)], axis=0)
+        chunks = (dot_t(place[...], gated) + dot(gather[...], rest)).astype(BF16)
+        for j in range(2):
+            at = (i + j) * peers * stride
+            out_ref[at : at + peers * stride, :] = chunks[:, j * block : (j + 1) * block]
 
     stores = []
     ahead = gate(0)
-    for i in range(steps):
+    for i in range(0, steps, 2):
         current = ahead
-        if i + 1 < steps:
-            ahead = gate(i + 1)
+        if i + 2 < steps:
+            ahead = gate(i + 2)
         put(i, *current)
-        to = pl.ds(i * peers * stride, peers * stride)
+        to = pl.ds(i * peers * stride, 2 * peers * stride)
         stores.append(copy(out_ref.at[to], out_hbm.at[to], sems.at[5 + i]))
         stores[-1].start()
 
@@ -115,10 +132,10 @@
     rows = pltpu.roll(rows, (channels - slot_of(lax.axis_index("ctx")) * width) % channels, 1)[:, :length]
     columns = rows.T[:width]
     lane = iota((width, length), 1)
-    mine = (lane + 2 + 8 * iota((width, length), 0)) % length < 8
+    mine = ((lane + 2 + 8 * iota((width, length), 0)) & (length - 1)) < 8
     parted = []
     for j in range(3):
-        both = jnp.where((lane + 2) % 8 < 4, columns[:, j : j + 1], columns[:, 3 + j : 4 + j])
+        both = jnp.where(((lane + 2) & 7) < 4, columns[:, j : j + 1], columns[:, 3 + j : 4 + j])
         parted.append(jnp.sum(jnp.where(mine, both, 0.0), axis=0, keepdims=True))
     weights_ref[...] = jnp.concatenate(parted + [jnp.zeros((5, length), F32)], axis=0)
     skip_ref[...] = jnp.broadcast_to(columns[:, 6:7], (width, length))
@@ -126,7 +143,7 @@
         c.wait()
 
 
-def conv_kernel(got_ref, weights_ref, skip_ref, out_ref):
+def conv_kernel(got_ref, weights_ref, skip_ref, out_hbm, out_ref, sem):
     parts, width, length = out_ref.shape
     pairs = parts // 2
     stride = width + EXTRA
@@ -136,7 +153,7 @@
     at = [i * stride + width + 1 for i in at_stretch]
     own = jnp.concatenate([got_ref[i : i + 1, :].astype(F32) for i in at], axis=0)
     last = jnp.concatenate([jnp.zeros((1, length), F32), own[: parts - 1]], axis=0)
-    joined = jnp.where((lane + 2) % 4 < 2, last, own)
+    joined = jnp.where(((lane + 2) & 3) < 2, last, own)
     short = (
         weights_ref[0:1, :] * joined
         + weights_ref[1:2, :] * pltpu.roll(joined, 1, 1)
@@ -182,10 +199,20 @@
         if b:
             term = jnp.concatenate([jnp.zeros((b * width, 2 * length), F32), term], axis=0)
         total = total + term
-    total = total.astype(BF16)
-    for i, stretch in enumerate(ORDER_OUT):
-        at = (stretch // 2) * width
-        out_ref[i] = total[at : at + width, (stretch % 2) * length : (stretch % 2 + 1) * length]
+        if b % FLUSH == FLUSH - 1:
+            done = total[(b + 1 - FLUSH) * width : (b + 1) * width].astype(BF16)
+            ready = []
+            for i, stretch in enumerate(ORDER_OUT):
+                at = stretch // 2 - (b + 1 - FLUSH)
+                if 0 <= at < FLUSH:
+                    lanes = slice((stretch % 2) * length, (stretch % 2 + 1) * length)
+                    out_ref[i] = done[at * width : (at + 1) * width, lanes]
+                    ready.append(i)
+            starts = [i for i in ready if i - 1 not in ready]
+            ends = [i + 1 for i in ready if i + 1 not in ready]
+            for i, j in zip(starts, ends):
+                pltpu.make_async_copy(out_ref.at[i:j], out_hbm.at[i:j], sem).start()
+    pltpu.make_async_copy(out_ref, out_hbm, sem).wait()
 
 
 def mix_kernel(back_ref, q_ref, out_ref):
@@ -253,6 +280,11 @@
             pltpu.VMEM(filter_taps.shape, BF16),
             pltpu.VMEM((1, channels), F32),
             pltpu.VMEM((parts * (width + EXTRA), length), BF16),
+            pltpu.VMEM((3 * length, length), BF16),
+            pltpu.VMEM((2 * length, length), BF16),
+            pltpu.VMEM((length, length), BF16),
+            pltpu.VMEM((length // width * (width + EXTRA), length), BF16),
+            pltpu.VMEM((length // width * (width + EXTRA), length + 2 * length // width), BF16),
             pltpu.SemaphoreType.DMA((5 + channels // length,)),
         ],
         interpret=INTERPRET,
@@ -264,9 +296,13 @@
     before = lax.ppermute(q_stream[:, -2:], "ctx", pairs)
     q_short = lax.optimization_barrier(short_conv(q_stream, before, short_taps[0]))
 
-    parted = call(
+    parted = pl.pallas_call(
         conv_kernel,
-        ((parts, width, length), BF16),
+        out_shape=jax.ShapeDtypeStruct((parts, width, length), BF16),
+        out_specs=pl.BlockSpec(memory_space=pl.ANY),
+        scratch_shapes=[pltpu.VMEM((parts, width, length), BF16), pltpu.SemaphoreType.DMA],
+        interpret=INTERPRET,
+        name="conv_kernel",
     )(near(got), near(weights), near(skip))
     back = exchange(parted, ORDER_OUT)
     return call(mix_kernel, ((channels, length), BF16), near=False)(near(back), near(q_short))

time: 31.4 us -> 31.2 us (level)
  no operation moved by 1% of the time
where the time goes in v5:
time: 31.2 us; the launch traced here: 30.8 us
  starting transfers between devices  19.9 us (64%)
  waiting for transfers between devices  5.02 us (16%)
  Pallas kernels  4.36 us (14%)
  local copies, waits for them, and re-layouts  0.92 us (3%)
  other arithmetic  0.55 us (2%)
    all_to_all x2, starting transfers between devices, exchange(): lax.all_to_all(chunks, 'ctx', split_axis=0, concat_axis=0, tiled=True, ax...  18 us
    all_to_all x2, waiting for transfers between devices, exchange(): lax.all_to_all(chunks, 'ctx', split_axis=0, concat_axis=0, tiled=True, ax...  5.01 us
    pallas_call x1, Pallas kernels, body(): pl.pallas_call(pack_kernel, out_shape=(jax.ShapeDtypeStruct((parts * (wid...  2.32 us
    ppermute x1, starting transfers between devices, body(): before = lax.ppermute(q_stream[:, -2:], 'ctx', pairs)  1.93 us
    pallas_call x1, Pallas kernels, body(): pl.pallas_call(conv_kernel, out_shape=jax.ShapeDtypeStruct((parts, width,...  1.36 us
    slice x1, local copies, waits for them, and re-layouts, short_conv(): weights[0][:, None] * joined[:, 2:]  0.82 us
    pallas_call x1, Pallas kernels, body(): call(mix_kernel, ((channels, length), BF16), near=False)  0.68 us
  transfers between devices with their start and end apart: 3, of which 2 were waited for; matrix products, arithmetic and copies ran while one was open for 5% of the time, Pallas kernels for 4%

profile of v5, /device:TPU:1, one launch (start us, length us, event | category | flops | bytes accessed | tf_op | source)
XLA Modules:
  0.0 30.8 jit_solution(10916873875519290217)
XLA Ops:
  0.0 2.3 %pack_kernel.1 = (bf16[576,128]{1,0:T(8,128)(2,1)}, f32[8,128]{1,0:T(8,128)S(1)}, f32[16,128]{1,0:T(8,128)S(1)}) custom-call(bf16[512,128]{1,0:T(8,128)(2,1)} %k_hbm.1, bf16[512,128]{1,0:T(8,128)(2,1)} %x_hbm.1, f32[3,3,512]{2,1,0:T(4,128)} %taps_hbm.1, bf16[32,128]{1,0:T(8,128)(2,1)} %lags_hbm.1, f32[1,512]{1,0:T(1,128)} %bitcast.11), custom_call_target="tpu_custom_call" | custom-call | tf_op jit(solution)/shard_map/pack_kernel/pallas_call | solution.py:263
  2.3 0.0 copy-start
  2.3 10.7 %all-to-all-start = ((bf16[32,9,2,128]{3,2,1,0:T(2,128)(2,1)}), bf16[32,9,2,128]{3,2,1,0:T(2,128)(2,1)S(1)}, u32[]{:S(2)}, u32[]{:S(2)}) async-start(bf16[32,9,2,128]{3,2,1,0:T(2,128)(2,1)} %bitcast.7), calls=%async_computation | async-start | bytes 294912 | tf_op jit(solution)/shard_map/all_to_all | solution.py:253
  13.0 0.0 copy-done
  13.1 0.1 slice.29
  13.2 1.9 %collective-permute-start = (bf16[512,2]{1,0:T(8,128)(2,1)S(1)}, bf16[512,2]{1,0:T(8,128)(2,1)S(1)}, u32[]{:S(2)}, u32[]{:S(2)}) collective-permute-start(bf16[512,2]{1,0:T(8,128)(2,1)S(1)} %slice.29), channel_id=1, source_target_pairs={{0,8},{8,16},{16,24},{24,32},{32,40},{40,48},{48,56},{56,64},{64,7... | collective-permute-start | bytes 6152 | tf_op jit(solution)/shard_map/ppermute | solution.py:296
  15.1 0.8 %fusion.2 = (f32[1,1,512]{2,1,0:T(1,128)S(1)}, f32[1,1,512]{2,1,0:T(1,128)S(1)}, f32[1,1,512]{2,1,0:T(1,128)S(1)}) fusion(f32[3,3,512]{2,1,0:T(4,128)} %taps_hbm.1), kind=kLoop, calls=%fused_computation.6 | loop fusion | bytes 12288 | tf_op jit(solution)/shard_map/slice | solution.py:246
  15.9 1.8 %all-to-all-done = bf16[32,9,2,128]{3,2,1,0:T(2,128)(2,1)S(1)} async-done(((bf16[32,9,2,128]{3,2,1,0:T(2,128)(2,1)}), bf16[32,9,2,128]{3,2,1,0:T(2,128)(2,1)S(1)}, u32[]{:S(2)}, u32[]{:S(2)}) %all-to-all-start) | async-done | bytes 147488 | tf_op jit(solution)/shard_map/all_to_all | solution.py:253
  17.7 1.4 %conv_kernel.1 = bf16[32,16,128]{2,1,0:T(8,128)(2,1)} custom-call(bf16[576,128]{1,0:T(8,128)(2,1)S(1)} %bitcast.6, f32[8,128]{1,0:T(8,128)S(1)} %get-tuple-element.9.weights_ref, f32[16,128]{1,0:T(8,128)S(1)} %get-tuple-element.10.skip_ref), custom_call_target="tpu_custom_call" | custom-call | tf_op jit(solution)/shard_map/conv_kernel/pallas_call | solution.py:299
  19.0 7.3 %all-to-all-start.1 = ((bf16[32,16,128]{2,1,0:T(8,128)(2,1)}), bf16[32,16,128]{2,1,0:T(8,128)(2,1)S(1)}, u32[]{:S(2)}, u32[]{:S(2)}) async-start(bf16[32,16,128]{2,1,0:T(8,128)(2,1)} %conv_kernel.1), calls=%async_computation.1 | async-start | bytes 262144 | tf_op jit(solution)/shard_map/all_to_all | solution.py:253
  26.3 0.0 collective-permute-done
  26.3 0.1 maximum_convert_fusion
  26.5 0.4 %fusion.q_ref = f32[512,128]{1,0:T(8,128)S(1)} fusion(f32[512,130]{1,0:T(8,128)S(1)} %maximum_convert_fusion, f32[512]{0:T(512)S(1)} %bitcast.9, f32[512]{0:T(512)S(1)} %bitcast.10, f32[512]{0:T(512)S(1)} %bitcast.8), kind=kLoop, calls=%fused_computation.1 | loop fusion | flops 327680 | bytes 1054720 | tf_op jit(solution)/shard_map/add | solution.py:246
  26.9 3.3 %all-to-all-done.1.back_ref = bf16[32,16,128]{2,1,0:T(8,128)(2,1)S(1)} async-done(((bf16[32,16,128]{2,1,0:T(8,128)(2,1)}), bf16[32,16,128]{2,1,0:T(8,128)(2,1)S(1)}, u32[]{:S(2)}, u32[]{:S(2)}) %all-to-all-start.1) | async-done | bytes 131104 | tf_op jit(solution)/shard_map/all_to_all | solution.py:253
  30.2 0.7 %mix_kernel.1 = bf16[512,128]{1,0:T(8,128)(2,1)} custom-call(bf16[32,16,128]{2,1,0:T(8,128)(2,1)S(1)} %all-to-all-done.1.back_ref, f32[512,128]{1,0:T(8,128)S(1)} %fusion.q_ref), custom_call_target="tpu_custom_call" | custom-call | tf_op jit(solution)/shard_map/mix_kernel/pallas_call | solution.py:308
Async XLA Ops:
  2.3 10.7 %copy-start = (bf16[512,128]{1,0:T(8,128)(2,1)S(1)}, bf16[512,128]{1,0:T(8,128)(2,1)}, u32[]{:S(2)}) copy-start(bf16[512,128]{1,0:T(8,128)(2,1)} %param.6) | copy-start | bytes 393220
  2.3 15.3 %all-to-all-start = ((bf16[32,9,2,128]{3,2,1,0:T(2,128)(2,1)}), bf16[32,9,2,128]{3,2,1,0:T(2,128)(2,1)S(1)}, u32[]{:S(2)}, u32[]{:S(2)}) async-start(bf16[32,9,2,128]{3,2,1,0:T(2,128)(2,1)} %bitcast.7), calls=%async_computation | async-start | bytes 294912 | tf_op jit(solution)/shard_map/all_to_all | solution.py:253
  13.2 13.2 %collective-permute-start = (bf16[512,2]{1,0:T(8,128)(2,1)S(1)}, bf16[512,2]{1,0:T(8,128)(2,1)S(1)}, u32[]{:S(2)}, u32[]{:S(2)}) collective-permute-start(bf16[512,2]{1,0:T(8,128)(2,1)S(1)} %slice.29), channel_id=1, source_target_pairs={{0,8},{8,16},{16,24},{24,32},{32,40},{40,48},{48,56},{56,64},{64,7... | collective-permute-start | bytes 6152 | tf_op jit(solution)/shard_map/ppermute | solution.py:296
  19.0 11.1 %all-to-all-start.1 = ((bf16[32,16,128]{2,1,0:T(8,128)(2,1)}), bf16[32,16,128]{2,1,0:T(8,128)(2,1)S(1)}, u32[]{:S(2)}, u32[]{:S(2)}) async-start(bf16[32,16,128]{2,1,0:T(8,128)(2,1)} %conv_kernel.1), calls=%async_computation.1 | async-start | bytes 262144 | tf_op jit(solution)/shard_map/all_to_all | solution.py:253

commit v6 on v5

--- a/solution.py
+++ b/solution.py
@@ -86,7 +86,7 @@
     lag = (col >= block) & (col < block + peers) & (row == stride * (col - block) + width)
     gather[...] = one_hot(sample | lag)
 
-    for c in loads:
+    for c in loads[:1] + loads[2:]:
         c.wait()
 
     def short(moved, m, i, at):
@@ -100,8 +100,10 @@
     def gate(i):
         rows = slice(i * block, (i + 2) * block)
         k = k_ref[rows, :]
+        moved_k = dot_t(shifts[...], k)
+        if i == 0:
+            loads[1].wait()
         x = x_ref[rows, :]
-        moved_k = dot_t(shifts[...], k)
         moved_x = dot_t(shifts[...], x)
         edges = dot(jnp.concatenate([k, x], axis=1), pick[...]).astype(BF16)
         gated = [short(moved_k, 1, i + j, j) * short(moved_x, 2, i + j, j) for j in range(2)]

time: 31.2 us -> 31.4 us (level)
  no operation moved by 1% of the time
where the time goes in v6:
time: 31.4 us; the launch traced here: 31 us
  starting transfers between devices  19.9 us (63%)
  waiting for transfers between devices  5.02 us (16%)
  Pallas kernels  4.55 us (14%)
  local copies, waits for them, and re-layouts  0.92 us (3%)
  other arithmetic  0.55 us (2%)
    all_to_all x2, starting transfers between devices, exchange(): lax.all_to_all(chunks, 'ctx', split_axis=0, concat_axis=0, tiled=True, ax...  18 us
    all_to_all x2, waiting for transfers between devices, exchange(): lax.all_to_all(chunks, 'ctx', split_axis=0, concat_axis=0, tiled=True, ax...  5.01 us
    pallas_call x1, Pallas kernels, body(): pl.pallas_call(pack_kernel, out_shape=(jax.ShapeDtypeStruct((parts * (wid...  2.5 us
    ppermute x1, starting transfers between devices, body(): before = lax.ppermute(q_stream[:, -2:], 'ctx', pairs)  1.93 us
    pallas_call x1, Pallas kernels, body(): pl.pallas_call(conv_kernel, out_shape=jax.ShapeDtypeStruct((parts, width,...  1.37 us
    slice x1, local copies, waits for them, and re-layouts, short_conv(): weights[0][:, None] * joined[:, 2:]  0.82 us
    pallas_call x1, Pallas kernels, body(): call(mix_kernel, ((channels, length), BF16), near=False)  0.68 us
  transfers between devices with their start and end apart: 3, of which 2 were waited for; matrix products, arithmetic and copies ran while one was open for 5% of the time, Pallas kernels for 4%

profile of v6, /device:TPU:1, one launch (start us, length us, event | category | flops | bytes accessed | tf_op | source)
XLA Modules:
  0.0 31.0 jit_solution(1093645244722960181)
XLA Ops:
  0.0 2.5 %pack_kernel.1 = (bf16[576,128]{1,0:T(8,128)(2,1)}, f32[8,128]{1,0:T(8,128)S(1)}, f32[16,128]{1,0:T(8,128)S(1)}) custom-call(bf16[512,128]{1,0:T(8,128)(2,1)} %k_hbm.1, bf16[512,128]{1,0:T(8,128)(2,1)} %x_hbm.1, f32[3,3,512]{2,1,0:T(4,128)} %taps_hbm.1, bf16[32,128]{1,0:T(8,128)(2,1)} %lags_hbm.1, f32[1,512]{1,0:T(1,128)} %bitcast.11), custom_call_target="tpu_custom_call" | custom-call | tf_op jit(solution)/shard_map/pack_kernel/pallas_call | solution.py:265
  2.5 0.0 copy-start
  2.5 10.7 %all-to-all-start = ((bf16[32,9,2,128]{3,2,1,0:T(2,128)(2,1)}), bf16[32,9,2,128]{3,2,1,0:T(2,128)(2,1)S(1)}, u32[]{:S(2)}, u32[]{:S(2)}) async-start(bf16[32,9,2,128]{3,2,1,0:T(2,128)(2,1)} %bitcast.7), calls=%async_computation | async-start | bytes 294912 | tf_op jit(solution)/shard_map/all_to_all | solution.py:255
  13.2 0.0 copy-done
  13.2 0.1 slice.29
  13.3 1.9 %collective-permute-start = (bf16[512,2]{1,0:T(8,128)(2,1)S(1)}, bf16[512,2]{1,0:T(8,128)(2,1)S(1)}, u32[]{:S(2)}, u32[]{:S(2)}) collective-permute-start(bf16[512,2]{1,0:T(8,128)(2,1)S(1)} %slice.29), channel_id=1, source_target_pairs={{0,8},{8,16},{16,24},{24,32},{32,40},{40,48},{48,56},{56,64},{64,7... | collective-permute-start | bytes 6152 | tf_op jit(solution)/shard_map/ppermute | solution.py:298
  15.3 0.8 %fusion.2 = (f32[1,1,512]{2,1,0:T(1,128)S(1)}, f32[1,1,512]{2,1,0:T(1,128)S(1)}, f32[1,1,512]{2,1,0:T(1,128)S(1)}) fusion(f32[3,3,512]{2,1,0:T(4,128)} %taps_hbm.1), kind=kLoop, calls=%fused_computation.6 | loop fusion | bytes 12288 | tf_op jit(solution)/shard_map/slice | solution.py:248
  16.1 1.8 %all-to-all-done = bf16[32,9,2,128]{3,2,1,0:T(2,128)(2,1)S(1)} async-done(((bf16[32,9,2,128]{3,2,1,0:T(2,128)(2,1)}), bf16[32,9,2,128]{3,2,1,0:T(2,128)(2,1)S(1)}, u32[]{:S(2)}, u32[]{:S(2)}) %all-to-all-start) | async-done | bytes 147488 | tf_op jit(solution)/shard_map/all_to_all | solution.py:255
  17.8 1.4 %conv_kernel.1 = bf16[32,16,128]{2,1,0:T(8,128)(2,1)} custom-call(bf16[576,128]{1,0:T(8,128)(2,1)S(1)} %bitcast.6, f32[8,128]{1,0:T(8,128)S(1)} %get-tuple-element.9.weights_ref, f32[16,128]{1,0:T(8,128)S(1)} %get-tuple-element.10.skip_ref), custom_call_target="tpu_custom_call" | custom-call | tf_op jit(solution)/shard_map/conv_kernel/pallas_call | solution.py:301
  19.2 7.3 %all-to-all-start.1 = ((bf16[32,16,128]{2,1,0:T(8,128)(2,1)}), bf16[32,16,128]{2,1,0:T(8,128)(2,1)S(1)}, u32[]{:S(2)}, u32[]{:S(2)}) async-start(bf16[32,16,128]{2,1,0:T(8,128)(2,1)} %conv_kernel.1), calls=%async_computation.1 | async-start | bytes 262144 | tf_op jit(solution)/shard_map/all_to_all | solution.py:255
  26.5 0.0 collective-permute-done
  26.5 0.1 maximum_convert_fusion
  26.7 0.4 %fusion.q_ref = f32[512,128]{1,0:T(8,128)S(1)} fusion(f32[512,130]{1,0:T(8,128)S(1)} %maximum_convert_fusion, f32[512]{0:T(512)S(1)} %bitcast.9, f32[512]{0:T(512)S(1)} %bitcast.10, f32[512]{0:T(512)S(1)} %bitcast.8), kind=kLoop, calls=%fused_computation.1 | loop fusion | flops 327680 | bytes 1054720 | tf_op jit(solution)/shard_map/add | solution.py:248
  27.1 3.3 %all-to-all-done.1.back_ref = bf16[32,16,128]{2,1,0:T(8,128)(2,1)S(1)} async-done(((bf16[32,16,128]{2,1,0:T(8,128)(2,1)}), bf16[32,16,128]{2,1,0:T(8,128)(2,1)S(1)}, u32[]{:S(2)}, u32[]{:S(2)}) %all-to-all-start.1) | async-done | bytes 131104 | tf_op jit(solution)/shard_map/all_to_all | solution.py:255
  30.3 0.7 %mix_kernel.1 = bf16[512,128]{1,0:T(8,128)(2,1)} custom-call(bf16[32,16,128]{2,1,0:T(8,128)(2,1)S(1)} %all-to-all-done.1.back_ref, f32[512,128]{1,0:T(8,128)S(1)} %fusion.q_ref), custom_call_target="tpu_custom_call" | custom-call | tf_op jit(solution)/shard_map/mix_kernel/pallas_call | solution.py:310
Async XLA Ops:
  2.5 10.7 %copy-start = (bf16[512,128]{1,0:T(8,128)(2,1)S(1)}, bf16[512,128]{1,0:T(8,128)(2,1)}, u32[]{:S(2)}) copy-start(bf16[512,128]{1,0:T(8,128)(2,1)} %param.6) | copy-start | bytes 393220
  2.5 15.3 %all-to-all-start = ((bf16[32,9,2,128]{3,2,1,0:T(2,128)(2,1)}), bf16[32,9,2,128]{3,2,1,0:T(2,128)(2,1)S(1)}, u32[]{:S(2)}, u32[]{:S(2)}) async-start(bf16[32,9,2,128]{3,2,1,0:T(2,128)(2,1)} %bitcast.7), calls=%async_computation | async-start | bytes 294912 | tf_op jit(solution)/shard_map/all_to_all | solution.py:255
  13.3 13.2 %collective-permute-start = (bf16[512,2]{1,0:T(8,128)(2,1)S(1)}, bf16[512,2]{1,0:T(8,128)(2,1)S(1)}, u32[]{:S(2)}, u32[]{:S(2)}) collective-permute-start(bf16[512,2]{1,0:T(8,128)(2,1)S(1)} %slice.29), channel_id=1, source_target_pairs={{0,8},{8,16},{16,24},{24,32},{32,40},{40,48},{48,56},{56,64},{64,7... | collective-permute-start | bytes 6152 | tf_op jit(solution)/shard_map/ppermute | solution.py:298
  19.2 11.1 %all-to-all-start.1 = ((bf16[32,16,128]{2,1,0:T(8,128)(2,1)}), bf16[32,16,128]{2,1,0:T(8,128)(2,1)S(1)}, u32[]{:S(2)}, u32[]{:S(2)}) async-start(bf16[32,16,128]{2,1,0:T(8,128)(2,1)} %conv_kernel.1), calls=%async_computation.1 | async-start | bytes 262144 | tf_op jit(solution)/shard_map/all_to_all | solution.py:255
